TPU v7x, 256 devices: a whole 4x4x8 slice. The times are simulated.
256 devices in a mesh: row: 16 (over z, core), col: 16 (over x, y).
Axes of the slice: x: 4, y: 4, z: 8, core: 2. Of those that a mesh axis runs over, the one named last changes fastest.
Arguments:
- source_emb: bfloat16 [65536, 256], P(('col', 'row')), may hold values from -6 to 6
- self_feat: bfloat16 [65536, 256], P(('row', 'col')), may hold values from -6 to 6
- w_self: bfloat16 [256, 256], replicated, may hold values from -0.375 to 0.375
- w_neigh: bfloat16 [256, 256], replicated, may hold values from -0.375 to 0.375
- bias: float32 [256], replicated, may hold values from -3 to 3
- cotangent: bfloat16 [65536, 256], P(('row', 'col')), may hold values from -6 to 6
- tile_dst: int32 [16, 16, 128], P('row', 'col'), may hold values from 0 to 31, as said below
- tile_src: int32 [16, 16, 128], P('row', 'col'), may hold values from 0 to 31
- tile_live: int32 [16, 16], P('row', 'col'), may hold values from 1 to 128, as said below
- tile_counts: int32 [16, 16, 128, 128, 128], P('row', 'col'), may hold values from 0 to 3, as said below
Outputs:
- layer_out: bfloat16 [65536, 256], P(('row', 'col'))
- grad_self: bfloat16 [65536, 256], P(('row', 'col'))
- grad_source: bfloat16 [65536, 256], P(('col', 'row'))
- grad_w_self: float32 [256, 256], replicated
- grad_w_neigh: float32 [256, 256], replicated
- grad_bias: float32 [256], replicated
Inputs may be any that keep to these rules, and one draw needn't show every extreme that they name: Within one grid cell the pairs (tile_dst, tile_src) of all 128 slots are distinct. `tile_live`: some grid cell uses all 128 slots in every draw. `tile_counts`: slots at or past tile_live hold counts too, which are ignored.
All inputs are finite; a program needn't handle non-finite values.
Results may differ from a plain program's by a relative error of at most 0.007.
Values may be sent and summed in bfloat16 or wider, within the bound.
A program may use at most 128 MiB of HBM per device.

v0:
```python
import math

import jax
import jax.numpy as jnp
from jax import lax
from jax.sharding import PartitionSpec as P


def block_terms(weights, table, pick_ids, target_ids, places, transpose):
    picked = jnp.take(table, pick_ids, axis=0)
    pattern = "tji,tjh->tih" if transpose else "tij,tjh->tih"
    tile_terms = jnp.einsum(pattern, weights, picked, preferred_element_type=jnp.float32)
    summed = jax.ops.segment_sum(tile_terms, target_ids, num_segments=places)
    return summed.reshape(places, -1)


def block_degree(weights, target_ids, places):
    row_counts = jnp.sum(weights.astype(jnp.float32), axis=2)
    return jax.ops.segment_sum(row_counts, target_ids, num_segments=places)


def body(
    source_emb,
    self_feat,
    w_self,
    w_neigh,
    bias,
    cotangent,
    tile_dst,
    tile_src,
    tile_live,
    tile_counts,
):
    tile_slots = tile_counts.shape[2]
    block_size = tile_counts.shape[3]
    feat_width = source_emb.shape[1]
    counts = tile_counts.reshape(tile_slots, block_size, block_size)
    dst_ids = tile_dst.reshape(tile_slots)
    src_ids = tile_src.reshape(tile_slots)
    live_count = tile_live.reshape(())
    slot_ids = jnp.arange(tile_slots, dtype=jnp.int32)
    weights = jnp.where(slot_ids[:, None, None] < live_count, counts, 0).astype(jnp.bfloat16)
    gathered = lax.all_gather(source_emb, "row", axis=0, tiled=True)
    src_rows = gathered.shape[0]
    src_blocks = src_rows // block_size
    dst_rows = self_feat.shape[0] * lax.axis_size("col")
    dst_blocks = dst_rows // block_size
    source_table = gathered.reshape(src_blocks, block_size, feat_width)
    summed = block_terms(weights, source_table, src_ids, dst_ids, dst_blocks, False)
    partial_degree = block_degree(weights, dst_ids, dst_blocks)
    neighbor_sum, degree = (
        lax.psum_scatter(
            summed.reshape(dst_rows, feat_width), "col", scatter_dimension=0, tiled=True
        ),
        lax.psum_scatter(partial_degree.reshape(dst_rows), "col", scatter_dimension=0, tiled=True),
    )
    inv_root = 1.0 / jnp.sqrt(degree + 1.0)
    aggregate = (neighbor_sum * inv_root[:, None]).astype(jnp.bfloat16)
    preact = (
        jnp.dot(self_feat, w_self, preferred_element_type=jnp.float32)
        + jnp.dot(aggregate, w_neigh, preferred_element_type=jnp.float32)
        + bias
    )
    layer_out = jax.nn.silu(preact).astype(jnp.bfloat16)
    sigmoid_z = jax.nn.sigmoid(preact)
    grad_pre = (
        cotangent.astype(jnp.float32) * sigmoid_z * (1.0 + preact * (1.0 - sigmoid_z))
    ).astype(jnp.bfloat16)
    local_self = jnp.dot(self_feat.T, grad_pre, preferred_element_type=jnp.float32)
    local_neigh = jnp.dot(aggregate.T, grad_pre, preferred_element_type=jnp.float32)
    local_bias = jnp.sum(grad_pre.astype(jnp.float32), axis=0)
    total_self, total_neigh, total_bias = lax.psum(
        (local_self, local_neigh, local_bias), ("row", "col")
    )
    scale = 1.0 / math.sqrt(self_feat.shape[0] * lax.axis_size("row") * lax.axis_size("col"))
    grad_self = jnp.dot(grad_pre, w_self.T, preferred_element_type=jnp.float32).astype(jnp.bfloat16)
    grad_sum = (
        jnp.dot(grad_pre, w_neigh.T, preferred_element_type=jnp.float32) * inv_root[:, None]
    ).astype(jnp.bfloat16)
    grad_slab = lax.all_gather(grad_sum, "col", axis=0, tiled=True)
    grad_table = grad_slab.reshape(dst_blocks, block_size, feat_width)
    back_sum = (block_terms(weights, grad_table, dst_ids, src_ids, src_blocks, True),)[0]
    grad_source = lax.psum_scatter(
        back_sum.reshape(src_rows, feat_width), "row", scatter_dimension=0, tiled=True
    ).astype(jnp.bfloat16)
    return (
        layer_out,
        grad_self,
        grad_source,
        total_self * scale,
        total_neigh * scale,
        total_bias * scale,
    )


def solution(mesh):
    in_specs = (
        P(("col", "row"), None),
        P(("row", "col"), None),
        P(),
        P(),
        P(),
        P(("row", "col"), None),
        P("row", "col", None),
        P("row", "col", None),
        P("row", "col"),
        P("row", "col", None, None, None),
    )
    out_specs = (
        P(("row", "col"), None),
        P(("row", "col"), None),
        P(("col", "row"), None),
        P(),
        P(),
        P(),
    )
    return jax.shard_map(body, mesh=mesh, in_specs=in_specs, out_specs=out_specs, check_vma=False)
```

profile of v0, /device:TPU:1, one launch (start us, length us, event | category | flops | bytes accessed | tf_op | source)
XLA Modules:
  0.0 576.8 jit_solution(789061130887495395)
XLA Ops:
  10.0 6.4 %convert_reduce_fusion = (f32[128,128]{1,0:T(8,128)S(1)}, bf16[128,128,128]{2,1,0:T(8,128)(2,1)}) fusion(s32[1,1,128,128,128]{4,3,2,1,0:T(8,128)} %param.21, pred[128]{0:T(512)(128)(4,1)S(1)} %iota_compare_fusion), kind=kLoop, calls=%fused_computation.11 | loop fusion | flops 8372224 | bytes 12648576 | tf_op jit(solution)/shard_map/reduce_sum | solution.py:18
  16.3 37.5 %all-gather.3.cloned.1.call-done = bf16[4096,256]{1,0:T(8,128)(2,1)} async-done(((bf16[256,256]{1,0:T(8,128)(2,1)}), bf16[4096,256]{1,0:T(8,128)(2,1)}) %all-gather.3.cloned.1.call-update) | async-done | bytes 2097168 | tf_op jit(solution)/shard_map/all_gather | solution.py:43
  53.8 8.2 %gather_fusion = bf16[128,128,256]{2,1,0:T(8,128)(2,1)} fusion(bf16[32,128,256]{2,1,0:T(8,128)(2,1)} %bitcast.38, s32[1024]{0:T(1024)S(1)} %pad_clamp_fusion.1), kind=kCustom, calls=%fused_computation.clone | custom fusion | bytes 16777728 | tf_op jit(solution)/shard_map/jit(_take)/gather | solution.py:10
  62.0 12.8 %fusion.3 = f32[128,128,256]{2,1,0:T(8,128)} fusion(bf16[128,128,128]{2,1,0:T(8,128)(2,1)} %get-tuple-element.24, bf16[128,128,256]{2,1,0:T(8,128)(2,1)} %gather_fusion, pred[128]{0:T(512)(128)(4,1)S(1)} %compare_and_fusion.1), kind=kOutput, calls=%fused_computation.9 | convolution fusion | flops 1077936128 | bytes 29360256 | tf_op jit(solution)/shard_map/tij,tjh->tih/dot_general | solution.py:12
  74.8 2.4 broadcast.22.clone
  77.2 38.1 %scatter_fusion = f32[32,128,256]{2,1,0:T(8,128)} fusion(f32[32,128,256]{2,1,0:T(8,128)} %broadcast.22.clone, s32[128]{0:T(128)S(1)} %bitcast.40, f32[128,128,256]{2,1,0:T(8,128)} %fusion.3), kind=kCustom, calls=%fused_computation.2 | custom fusion | flops 4194304 | bytes 50332160 | tf_op jit(solution)/shard_map/scatter-add | solution.py:13
  116.6 1.0 scatter_custom_fusion.1
  117.6 59.8 %all-reduce = f32[4096]{0:T(1024)S(1)} all-reduce(f32[4096]{0:T(1024)S(1)} %bitcast.39), channel_id=3, replica_groups=mesh['row'=16,'col'=16] {'col'}, use_global_device_ids=true, to_apply=%region_4.6.clone | all-reduce | flops 4096 | bytes 32768
  177.7 16.8 %reduce-scatter.3.cloned.1.call-done = f32[256,256]{1,0:T(8,128)} async-done(((f32[4096,256]{1,0:T(8,128)}), f32[256,256]{1,0:T(8,128)}) %reduce-scatter.3.cloned.1.call-update) | async-done | bytes 262160 | tf_op jit(solution)/shard_map/reduce_scatter | solution.py:52
  194.5 1.9 convert_reduce_fusion.1
  196.5 0.9 fusion.10
  197.5 0.9 convolution_bitcast_fusion
  198.4 1.9 fusion.16
  200.6 47.5 %all-gather.5.cloned.1.call-done = bf16[4096,256]{1,0:T(8,128)(2,1)} async-done(((bf16[256,256]{1,0:T(8,128)(2,1)}), bf16[4096,256]{1,0:T(8,128)(2,1)}) %all-gather.5.cloned.1.call-update) | async-done | bytes 2097168 | tf_op jit(solution)/shard_map/all_gather | solution.py:80
  248.0 8.2 %gather_fusion.1 = bf16[128,128,256]{2,1,0:T(8,128)(2,1)} fusion(bf16[32,128,256]{2,1,0:T(8,128)(2,1)} %bitcast.37, s32[1024]{0:T(1024)S(1)} %pad_clamp_fusion), kind=kCustom, calls=%fused_computation.1.clone | custom fusion | bytes 16777728 | tf_op jit(solution)/shard_map/jit(_take)/gather | solution.py:10
  256.2 12.9 %fusion.1 = f32[128,128,256]{2,1,0:T(8,128)} fusion(bf16[128,128,128]{2,1,0:T(8,128)(2,1)} %get-tuple-element.24, bf16[128,128,256]{2,1,0:T(8,128)(2,1)} %gather_fusion.1, pred[128]{0:T(512)(128)(4,1)S(1)} %compare_and_fusion), kind=kOutput, calls=%fused_computation.7 | convolution fusion | flops 1077936128 | bytes 29360256 | tf_op jit(solution)/shard_map/tji,tjh->tih/dot_general | solution.py:12
  269.1 2.4 broadcast.22
  271.5 38.0 %scatter_fusion.1 = f32[32,128,256]{2,1,0:T(8,128)} fusion(f32[32,128,256]{2,1,0:T(8,128)} %broadcast.22, s32[128]{0:T(128)S(1)} %bitcast.42, f32[128,128,256]{2,1,0:T(8,128)} %fusion.1), kind=kCustom, calls=%fused_computation.4 | custom fusion | flops 4194304 | bytes 50332160 | tf_op jit(solution)/shard_map/scatter-add | solution.py:13
  309.5 77.0 %psum.23 = f32[256]{0:T(256)S(1)} all-reduce(f32[256]{0:T(256)S(1)} %get-tuple-element.21), channel_id=1, replica_groups=mesh['row'=16,'col'=16] {'row','col'}, use_global_device_ids=true, to_apply=%region_10.12 | all-reduce | flops 256 | bytes 2048 | tf_op jit(solution)/shard_map/psum | solution.py:72
  387.1 0.9 convolution_convert_fusion
  388.0 118.3 %all-reduce.4.cloned.1.call-done = (f32[256,256]{0,1:T(8,128)}, f32[256,256]{0,1:T(8,128)}) async-done(((f32[256,256]{0,1:T(8,128)}, f32[256,256]{0,1:T(8,128)}), (f32[256,256]{0,1:T(8,128)}, f32[256,256]{0,1:T(8,128)})) %all-reduce.4.cloned.1.call-update) | async-done | bytes 524304 | tf_op jit(solution)/shard_map/psum | solution.py:72
  506.3 1.1 broadcast_multiply_fusion
  509.0 59.6 %reduce-scatter.5.cloned.1.call-done = f32[256,256]{1,0:T(8,128)} async-done(((f32[4096,256]{1,0:T(8,128)}), f32[256,256]{1,0:T(8,128)}) %reduce-scatter.5.cloned.1.call-update) | async-done | bytes 262160 | tf_op jit(solution)/shard_map/reduce_scatter | solution.py:83
  568.6 1.6 convert_element_type.38
  (41 shorter events, 5.6 us)
Async XLA Ops:
  7.2 187.4 %copy-start = (bf16[256,256]{1,0:T(8,128)(2,1)S(1)}, bf16[256,256]{1,0:T(8,128)(2,1)}, u32[]{:S(2)}) copy-start(bf16[256,256]{1,0:T(8,128)(2,1)} %param.15) | copy-start | bytes 393220
  7.2 46.6 %all-gather.3.cloned.1.call-start = ((), (), s32[]{:S(2)}) async-start(), calls=%async_computation.2 | async-start | bytes 2228224 | tf_op jit(solution)/shard_map/all_gather | solution.py:43
  7.9 186.6 %reduce-scatter.3.cloned.1.call-start = ((), (), s32[]{:S(2)}) async-start(), calls=%async_computation.3 | async-start | bytes 4456448 | tf_op jit(solution)/shard_map/reduce_scatter | solution.py:52
  62.0 15.2 %copy-start.4 = (s32[1,1,128]{2,1,0:T(1,128)S(1)}, s32[1,1,128]{2,1,0:T(1,128)}, u32[]{:S(2)}) copy-start(s32[1,1,128]{2,1,0:T(1,128)} %param.18) | copy-start | bytes 1540
  77.2 38.2 %copy-start.8 = (u32[256]{0:T(256)S(1)}, u32[256]{0:T(256)}, u32[]{:S(2)}) copy-start(u32[256]{0:T(256)} %constant.30) | copy-start | bytes 3076
  77.2 100.3 %copy-start.2 = (bf16[256,256]{1,0:T(8,128)(2,1)S(1)}, bf16[256,256]{1,0:T(8,128)(2,1)}, u32[]{:S(2)}) copy-start(bf16[256,256]{1,0:T(8,128)(2,1)} %param.14) | copy-start | bytes 393220
  77.2 100.3 %copy-start.3 = (bf16[256,256]{1,0:T(8,128)(2,1)S(1)}, bf16[256,256]{1,0:T(8,128)(2,1)}, u32[]{:S(2)}) copy-start(bf16[256,256]{1,0:T(8,128)(2,1)} %param.13) | copy-start | bytes 393220
  77.2 117.3 %copy-start.6 = (bf16[256,256]{1,0:T(8,128)(2,1)S(1)}, bf16[256,256]{1,0:T(8,128)(2,1)}, u32[]{:S(2)}) copy-start(bf16[256,256]{1,0:T(8,128)(2,1)} %param.17) | copy-start | bytes 393220
  77.2 117.3 %copy-start.7 = (f32[256]{0:T(256)S(1)}, f32[256]{0:T(256)}, u32[]{:S(2)}) copy-start(f32[256]{0:T(256)} %param.16) | copy-start | bytes 3076
  115.3 132.7 %all-gather.5.cloned.1.call-start = ((), (), s32[]{:S(2)}) async-start(), calls=%async_computation.4 | async-start | bytes 2228224 | tf_op jit(solution)/shard_map/all_gather | solution.py:80
  197.4 308.9 %all-reduce.4.cloned.1.call-start = ((), (), s32[]{:S(2)}) async-start(), calls=%async_computation.6 | async-start | bytes 1048576 | tf_op jit(solution)/shard_map/psum | solution.py:72
  200.3 368.3 %reduce-scatter.5.cloned.1.call-start = ((), (), s32[]{:S(2)}) async-start(), calls=%async_computation.5 | async-start | bytes 4456448 | tf_op jit(solution)/shard_map/reduce_scatter | solution.py:83
  256.2 15.3 %copy-start.5 = (s32[1,1,128]{2,1,0:T(1,128)S(1)}, s32[1,1,128]{2,1,0:T(1,128)}, u32[]{:S(2)}) copy-start(s32[1,1,128]{2,1,0:T(1,128)} %param.19) | copy-start | bytes 1540
  271.5 298.7 %copy-start.1 = (bf16[256,256]{1,0:T(8,128)(2,1)S(1)}, bf16[256,256]{1,0:T(8,128)(2,1)}, u32[]{:S(2)}) copy-start(bf16[256,256]{1,0:T(8,128)(2,1)} %param.15) | copy-start | bytes 393220
Sparse Core Ops, SparseCore 0:
  9.8 43.9 all-gather.2
  115.5 79.0 reduce-scatter.2
  197.8 50.1 all-gather.4
  255.0 251.1 all-reduce.3
  508.8 59.7 reduce-scatter.4
where the time goes:
time: 580 us; the launch traced here: 577 us
  waiting for transfers between devices  280 us (48%)
  blocking collectives  137 us (24%)
  other arithmetic  88.1 us (15%)
  matrix products  32.4 us (6%)
  local copies, waits for them, and re-layouts  23.4 us (4%)
  between operations  15.2 us (3%)
    psum x1, waiting for transfers between devices, body(): lax.psum((local_self, local_neigh, local_bias), ('row', 'col'))  118 us
    psum x1, blocking collectives, body(): lax.psum((local_self, local_neigh, local_bias), ('row', 'col'))  77 us
    scatter-add x2, other arithmetic, block_terms(): summed = jax.ops.segment_sum(tile_terms, target_ids, num_segments=places)  76 us
    unnamed x1, blocking collectives  59.8 us
    reduce_scatter x1, waiting for transfers between devices, body(): lax.psum_scatter(back_sum.reshape(src_rows, feat_width), 'row', scatter_d...  59.6 us
    all_gather x1, waiting for transfers between devices, body(): grad_slab = lax.all_gather(grad_sum, 'col', axis=0, tiled=True)  47.5 us
    all_gather x1, waiting for transfers between devices, body(): gathered = lax.all_gather(source_emb, 'row', axis=0, tiled=True)  37.5 us
    dot_general x2, matrix products, block_terms(): jnp.einsum(pattern, weights, picked, preferred_element_type=jnp.float32)  25.7 us
  transfers between devices with their start and end apart: 5, of which 5 were waited for; matrix products, arithmetic and copies ran while one was open for 14% of the time, Pallas kernels for 0%

commit v1 on v0

v1 whole, which is shorter than its diff:
```python
import functools
import math

import jax
import jax.numpy as jnp
from jax import lax
from jax.experimental import pallas as pl
from jax.experimental.pallas import tpu as pltpu
from jax.sharding import PartitionSpec as P

F32, BF16 = jnp.float32, jnp.bfloat16
MESH = pl.DeviceIdType.MESH
NZ, NX, NY = 8, 4, 4
NB = 32
SLOTS = 128
ZERO_SLOT = SLOTS


def rcopy(src, dst, ssem, rsem, **where):
    return pltpu.make_async_remote_copy(
        src_ref=src, dst_ref=dst, send_sem=ssem, recv_sem=rsem, device_id=where, device_id_type=MESH
    )


def kernel(
    scale,
    sel, dkey, emb, feat, w_self, w_neigh, bias, cot, counts,
    layer_out, grad_self, grad_source, g_ws, g_wn, g_b,
    stage, cnt, cnt_t, acc, tab, sa, sb, ra, rb, s2a, s2b, r2a, r2b, nsum, rsum, dg0, dg1, dg2, dg3,
    agg, gpre, dtab, ws1, wr1, ws2, wr2, wps, wpr, wz, wg, psend, precv, usend, urecv, dsend, drecv,
    csem, ag_r, ag_su, ag_sd, ag_sp, sa_s, sa_r, sb_s, sb_r, s2a_s, s2a_r, s2b_s, s2b_r,
    dgx_s, dgx_r, dgy_s, dgy_r, df_s, df_r, da_s, da_r, db_s, db_r,
    w1_s, w1_r, w2_s, w2_r, wp_s, wp_r, wz_s, wz_r, wy_s, wy_r, wx_s, wx_r,
    p_s, p_r, u_s, u_r, d_s, d_r,
):
    me_r, me_c = lax.axis_index("row"), lax.axis_index("col")
    z, k = me_r // 2, me_r % 2
    x, y = me_c // NY, me_c % NY
    kp = 1 - k

    def zm(v):
        return (v + 2 * NZ) % NZ

    def rw(zz, kk):
        return zm(zz) * 2 + kk

    def xm(j):
        return (x + j) % NX

    def ym(j):
        return (y + j) % NY

    def cl(xx, yy):
        return xx * NY + yy

    partner = rw(z, kp)

    def count_copy(i):
        part = pl.ds(i * 8, 8)
        return pltpu.make_async_copy(counts.at[part], stage.at[part], csem.at[i])

    def start_counts(i, carry):
        count_copy(i).start()
        return carry

    lax.fori_loop(0, 16, start_counts, 0)

    barrier = pltpu.get_barrier_semaphore()

    def greet_z(j, carry):
        pl.semaphore_signal(barrier, inc=1, device_id={"row": rw(z + j, k)}, device_id_type=MESH)
        return carry

    def greet_xy(j, carry):
        pl.semaphore_signal(barrier, inc=1, device_id={"col": cl(xm(j), y)}, device_id_type=MESH)
        pl.semaphore_signal(barrier, inc=1, device_id={"col": cl(x, ym(j))}, device_id_type=MESH)
        return carry

    pl.semaphore_signal(barrier, inc=1, device_id={"row": partner}, device_id_type=MESH)
    lax.fori_loop(1, NZ, greet_z, 0)
    lax.fori_loop(1, NX, greet_xy, 0)
    pl.semaphore_wait(barrier, 1 + (NZ - 1) + 2 * (NX - 1))

    def ag_up(src, r, u):
        return rcopy(src, tab.at[r], ag_su.at[u], ag_r.at[r], row=rw(z + 1, k))

    def ag_down(src, r, u):
        return rcopy(src, tab.at[r], ag_sd.at[u], ag_r.at[r], row=rw(z - 1, k))

    def ag_partner(src, r):
        return rcopy(src, tab.at[r], ag_sp.at[r // 2], ag_r.at[r], row=partner)

    def ag_wait(r):
        rcopy(tab.at[r], tab.at[r], ag_sp.at[r // 2], ag_r.at[r], row=partner).wait_recv()

    ag_up(emb, me_r, 0).start()
    ag_down(emb, me_r, 0).start()
    ag_partner(emb, me_r).start()
    tab[me_r] = emb[...]
    cnt[ZERO_SLOT] = jnp.zeros((128, 128), BF16)
    cnt_t[ZERO_SLOT] = jnp.zeros((128, 128), BF16)

    def zero_acc(i, carry):
        acc[pl.ds(pl.multiple_of(i * 256, 256), 256), :] = jnp.zeros((256, 256), F32)
        return carry

    lax.fori_loop(0, 16, zero_acc, 0)

    def convert(i, carry):
        count_copy(i).wait()
        part = pl.ds(i * 8, 8)
        cnt[part] = stage[part].astype(F32).astype(BF16)
        return carry

    lax.fori_loop(0, 16, convert, 0)

    def spmm(tiles, table, s0, s1, place):
        def block(b, carry):
            rows = []
            for i in range(8):
                d = b * 8 + i
                rows.append(
                    jnp.concatenate(
                        [
                            tiles[sel[place(d, 2 * s0)]],
                            tiles[sel[place(d, 2 * s0 + 1)]],
                            tiles[sel[place(d, 2 * s1)]],
                            tiles[sel[place(d, 2 * s1 + 1)]],
                        ],
                        axis=1,
                    )
                )
            lhs = jnp.concatenate(rows, axis=0)
            rhs = jnp.concatenate([table[s0], table[s1]], axis=0)
            r = pl.ds(pl.multiple_of(b * 1024, 1024), 1024)
            acc[r, :] += jnp.dot(lhs, rhs, preferred_element_type=F32)
            return carry

        lax.fori_loop(0, NB // 8, block, 0)

    def fwd_place(d, s):
        return d * NB + s

    def bwd_place(s, d):
        return d * NB + s

    def ag_step(t, carry):
        up, down = rw(z - t - 1, k), rw(z + t + 1, k)
        ag_wait(up)

        @pl.when(t < 3)
        def _():
            ag_up(tab.at[up], up, t + 1).start()

        ag_partner(tab.at[up], up).start()

        @pl.when(t < 3)
        def _():
            ag_wait(down)

            @pl.when(t < 2)
            def _():
                ag_down(tab.at[down], down, t + 1).start()

            ag_partner(tab.at[down], down).start()
            ag_wait(rw(z - t, kp))

        @pl.when(t == 3)
        def _():
            ag_wait(rw(z - t, kp))

        @pl.when(t > 0)
        def _():
            ag_wait(rw(z + t, kp))

        spmm(cnt, tab, rw(z - t, (k + (t + 3) // 4) % 2), rw(z + t, kp), fwd_place)

        @pl.when(t == 3)
        def _():
            ag_wait(rw(z - 4, kp))

        spmm(cnt, tab, up, rw(z + t + 1, (k + (t + 1) // 4) % 2), fwd_place)
        return carry

    lax.fori_loop(0, 4, ag_step, 0)

    def send_a(j):
        return rcopy(sa.at[xm(j)], ra.at[x], sa_s.at[j], sa_r.at[x], col=cl(xm(j), y))

    def send_b(j):
        return rcopy(sb.at[ym(j)], rb.at[y], sb_s.at[j], sb_r.at[y], col=cl(x, ym(j)))

    def emit(i, carry):
        jx, yy = (i // 4) + 1, i % 4
        xx = xm(jx)
        r = pl.ds(pl.multiple_of(cl(xx, yy) * 256, 256), 256)
        sa[xx, yy] = acc[r, 0:128].astype(BF16)
        sb[yy, xx] = acc[r, 128:256].astype(BF16)

        @pl.when((i % 4 == 3) & (i < 12))
        def _():
            send_a(jx).start()

        return carry

    lax.fori_loop(0, 16, emit, 0)

    def start_b(j, carry):
        send_b(j).start()
        return carry

    lax.fori_loop(1, NY, start_b, 0)

    def transpose(i, carry):
        t = cnt[i].T
        cnt_t[i] = t
        rsum[pl.ds(i, 1), :] = jnp.sum(t.astype(F32), axis=0, keepdims=True)
        return carry

    lax.fori_loop(0, SLOTS, transpose, 0)
    line = lax.broadcasted_iota(jnp.int32, (128, 128), 0)
    lane = lax.broadcasted_iota(jnp.int32, (128, 128), 1)
    hot = ((line // 8) * 2 + line % 8 == dkey[...]) & (line % 8 < 2)
    hot = jnp.where(hot, 1.0, 0.0).astype(BF16)
    part_a = jnp.minimum(rsum[...], 256.0)
    part_b = rsum[...] - part_a
    part_deg = jnp.dot(hot, part_a.astype(BF16), preferred_element_type=F32) + jnp.dot(
        hot, part_b.astype(BF16), preferred_element_type=F32
    )
    dg0[...] = part_deg.reshape(NX, NY, 8, 128)

    def send_dx(j):
        return rcopy(dg0.at[xm(j)], dg1.at[x], dgx_s.at[j], dgx_r.at[x], col=cl(xm(j), y))

    def send_dy(j):
        return rcopy(dg2.at[ym(j)], dg3.at[y], dgy_s.at[j], dgy_r.at[y], col=cl(x, ym(j)))

    for j in range(1, NX):
        send_dx(j).start()
    lax.fori_loop(0, 16, zero_acc, 0)
    dg1[x] = dg0[x]
    for j in range(1, NX):
        rcopy(dg1.at[xm(j)], dg1.at[xm(j)], dgx_s.at[j], dgx_r.at[xm(j)], col=me_c).wait_recv()
    dg2[...] = dg1[0] + dg1[1] + dg1[2] + dg1[3]
    for j in range(1, NY):
        send_dy(j).start()

    def send_a2(j):
        return rcopy(s2a.at[ym(j)], r2a.at[y], s2a_s.at[j], s2a_r.at[y], col=cl(x, ym(j)))

    def send_b2(j):
        return rcopy(s2b.at[xm(j)], r2b.at[x], s2b_s.at[j], s2b_r.at[x], col=cl(xm(j), y))

    for j in range(1, NX):
        rcopy(ra.at[xm(j)], ra.at[xm(j)], sa_s.at[j], sa_r.at[xm(j)], col=me_c).wait_recv()

    def sum_a(yy):
        return (
            sa[x, yy].astype(F32)
            + ra[xm(1), yy].astype(F32)
            + ra[xm(2), yy].astype(F32)
            + ra[xm(3), yy].astype(F32)
        )

    def sum_b(xx):
        return (
            sb[y, xx].astype(F32)
            + rb[ym(1), xx].astype(F32)
            + rb[ym(2), xx].astype(F32)
            + rb[ym(3), xx].astype(F32)
        )

    def stage_a2(j, carry):
        s2a[ym(j)] = sum_a(ym(j)).astype(BF16)
        send_a2(j).start()
        return carry

    lax.fori_loop(1, NY, stage_a2, 0)

    for j in range(1, NY):
        rcopy(rb.at[ym(j)], rb.at[ym(j)], sb_s.at[j], sb_r.at[ym(j)], col=me_c).wait_recv()

    def stage_b2(j, carry):
        s2b[xm(j)] = sum_b(xm(j)).astype(BF16)
        send_b2(j).start()
        return carry

    lax.fori_loop(1, NX, stage_b2, 0)
    nsum[:, 0:128] = sum_a(y)
    nsum[:, 128:256] = sum_b(x)

    dg3[y] = dg2[y]
    for j in range(1, NY):
        rcopy(dg3.at[ym(j)], dg3.at[ym(j)], dgy_s.at[j], dgy_r.at[ym(j)], col=me_c).wait_recv()
    degree = dg3[0] + dg3[1] + dg3[2] + dg3[3]
    inv_lane = 1.0 / jnp.sqrt(degree + 1.0)
    eye = line == lane
    inv_col = jnp.concatenate(
        [
            jnp.sum(jnp.where(eye, inv_lane[b : b + 1, :], 0.0), axis=1, keepdims=True)
            for b in range(2)
        ],
        axis=0,
    )

    for j in range(1, NY):
        rcopy(r2a.at[ym(j)], r2a.at[ym(j)], s2a_s.at[j], s2a_r.at[ym(j)], col=me_c).wait_recv()
    nsum[:, 0:128] += (
        r2a[ym(1)].astype(F32) + r2a[ym(2)].astype(F32) + r2a[ym(3)].astype(F32)
    )
    for j in range(1, NX):
        rcopy(r2b.at[xm(j)], r2b.at[xm(j)], s2b_s.at[j], s2b_r.at[xm(j)], col=me_c).wait_recv()
    nsum[:, 128:256] += (
        r2b[xm(1)].astype(F32) + r2b[xm(2)].astype(F32) + r2b[xm(3)].astype(F32)
    )

    agg[...] = (nsum[...] * inv_col).astype(BF16)
    pre = (
        jnp.dot(feat[...], w_self[...], preferred_element_type=F32)
        + jnp.dot(agg[...], w_neigh[...], preferred_element_type=F32)
        + bias[...]
    )
    sig = jax.nn.sigmoid(pre)
    layer_out[...] = (pre * sig).astype(BF16)
    gpre[...] = (cot[...].astype(F32) * sig * (1.0 + pre * (1.0 - sig))).astype(BF16)
    nt = (((1,), (1,)), ((), ()))
    tn = (((0,), (0,)), ((), ()))
    dtab[me_c] = (
        lax.dot_general(gpre[...], w_neigh[...], nt, preferred_element_type=F32) * inv_col
    ).astype(BF16)

    def full_x(j):
        return rcopy(dtab.at[me_c], dtab.at[me_c], df_s.at[j], df_r.at[me_c], col=cl(xm(j), y))

    def full_y(j):
        return rcopy(dtab.at[me_c], dtab.at[me_c], df_s.at[3 + j], df_r.at[me_c], col=cl(x, ym(j)))

    def half_a(jx, jy):
        part = dtab.at[cl(xm(jx), y), :, pl.ds(0, 128)]
        return rcopy(
            part, part, da_s.at[jx * 4 + jy], da_r.at[cl(xm(jx), y)], col=cl(x, ym(jy))
        )

    def half_b(jx, jy):
        part = dtab.at[cl(x, ym(jy)), :, pl.ds(128, 128)]
        return rcopy(
            part, part, db_s.at[jx * 4 + jy], db_r.at[cl(x, ym(jy))], col=cl(xm(jx), y)
        )

    def start_full(j, carry):
        full_x(j).start()
        full_y(j).start()
        return carry

    lax.fori_loop(1, 4, start_full, 0)

    grad_self[...] = lax.dot_general(
        gpre[...], w_self[...], nt, preferred_element_type=F32
    ).astype(BF16)
    gw = lax.dot_general(feat[...], gpre[...], tn, preferred_element_type=F32).astype(BF16)
    ws1[0, 0:128, :] = gw[0:128]
    ws1[1, 0:128, :] = gw[128:256]
    gw = lax.dot_general(agg[...], gpre[...], tn, preferred_element_type=F32).astype(BF16)
    ws1[2, 0:128, :] = gw[0:128]
    ws1[3, 0:128, :] = gw[128:256]
    gb = jnp.broadcast_to(jnp.sum(gpre[...].astype(F32), axis=0, keepdims=True), (16, 256))
    for j in range(4):
        ws1[j, 128:144, :] = gb.astype(BF16)

    def send_w1(j):
        return rcopy(ws1.at[xm(j)], wr1.at[x], w1_s.at[j], w1_r.at[x], col=cl(xm(j), y))

    def send_w2(j):
        return rcopy(ws2.at[ym(j)], wr2.at[y], w2_s.at[j], w2_r.at[y], col=cl(x, ym(j)))

    def send_wp():
        return rcopy(wps, wpr, wp_s, wp_r, row=partner)

    def send_wz(j):
        return rcopy(wz.at[z], wz.at[z], wz_s.at[j], wz_r.at[z], row=rw(z + j, k))

    def send_wy(j):
        return rcopy(wg.at[x, y], wg.at[x, y], wy_s.at[j], wy_r.at[y], col=cl(x, ym(j)))

    def send_wx(j):
        return rcopy(wg.at[x], wg.at[x], wx_s.at[j], wx_r.at[x], col=cl(xm(j), y))

    for j in range(1, NX):
        send_w1(j).start()
    wr1[x] = ws1[x]

    def take_x(jx):
        c = cl(xm(jx), y)
        rcopy(dtab.at[c], dtab.at[c], df_s.at[jx], df_r.at[c], col=me_c).wait_recv()

        def go(jy, carry):
            half_a(jx, jy).start()
            return carry

        lax.fori_loop(1, 4, go, 0)

    def take_y(jy):
        c = cl(x, ym(jy))
        rcopy(dtab.at[c], dtab.at[c], df_s.at[jy], df_r.at[c], col=me_c).wait_recv()

        def go(jx, carry):
            half_b(jx, jy).start()
            return carry

        lax.fori_loop(1, 4, go, 0)

    def take_rest(c):
        part = dtab.at[c, :, pl.ds(0, 128)]
        rcopy(part, part, da_s.at[0], da_r.at[c], col=me_c).wait_recv()
        part = dtab.at[c, :, pl.ds(128, 128)]
        rcopy(part, part, db_s.at[0], db_r.at[c], col=me_c).wait_recv()

    take_x(1)
    take_y(1)
    take_x(3)
    take_y(3)

    def order(q):
        m = q - 7
        dx = jnp.where(q < 4, q, jnp.where(q < 7, 0, 1 + m // 3))
        dy = jnp.where(q < 4, 0, jnp.where(q < 7, q - 3, 1 + m % 3))
        return cl(xm(dx), ym(dy))

    def bwd_step(g, carry):
        @pl.when(g == 1)
        def _():
            take_x(2)
            take_y(2)

        @pl.when(g == 2)
        def _():
            for j in range(1, NX):
                rcopy(wr1.at[xm(j)], wr1.at[xm(j)], w1_s.at[j], w1_r.at[xm(j)], col=me_c).wait_recv()
            tot = (
                wr1[0].astype(F32) + wr1[1].astype(F32) + wr1[2].astype(F32) + wr1[3].astype(F32)
            )
            for j in range(4):
                ws2[j, 0:32, :] = tot[j * 32 : j * 32 + 32]
                ws2[j, 32:40, :] = tot[128:136]
            for j in range(1, NY):
                send_w2(j).start()
            wr2[y] = ws2[y]

        @pl.when(g == 4)
        def _():
            for j in range(1, NY):
                rcopy(wr2.at[ym(j)], wr2.at[ym(j)], w2_s.at[j], w2_r.at[ym(j)], col=me_c).wait_recv()
            wps[...] = wr2[0] + wr2[1] + wr2[2] + wr2[3]
            send_wp().start()

        @pl.when(g == 5)
        def _():
            send_wp().wait_recv()
            wz[z] = wps[...] + wpr[...]
            for j in range(1, NZ):
                send_wz(j).start()

        @pl.when(g == 7)
        def _():
            for j in range(1, NZ):
                zz = zm(z + j)
                rcopy(wz.at[zz], wz.at[zz], wz_s.at[j], wz_r.at[zz], row=me_r).wait_recv()
            tot = wz[0]
            for j in range(1, NZ):
                tot = tot + wz[j]
            g_b[...] = tot[32:33] * scale
            wg[x, y] = tot[0:32]
            for j in range(1, NY):
                send_wy(j).start()

        @pl.when(g > 3)
        def _():
            take_rest(order(2 * g))

        @pl.when(g > 2)
        def _():
            take_rest(order(2 * g + 1))

        spmm(cnt_t, dtab, order(2 * g), order(2 * g + 1), bwd_place)
        return carry

    lax.fori_loop(0, 8, bwd_step, 0)

    def chunk(zz, kk):
        return acc[pl.ds(pl.multiple_of(rw(zz, kk) * 256, 256), 256), :]

    def send_p(zz):
        return rcopy(psend.at[zz], precv.at[zz], p_s.at[zz], p_r.at[zz], row=partner)

    def put_p(zz):
        psend[zz] = chunk(zz, kp).astype(BF16)
        send_p(zz).start()

    def emit_p(t, carry):
        put_p(zm(z + 4 - t))

        @pl.when(t < 3)
        def _():
            put_p(zm(z + 5 + t))

        return carry

    lax.fori_loop(0, 4, emit_p, 0)
    put_p(z)

    def send_u(t):
        return rcopy(usend.at[t], urecv.at[t], u_s.at[t], u_r.at[t], row=rw(z + 1, k))

    def send_d(t):
        return rcopy(dsend.at[t], drecv.at[t], d_s.at[t], d_r.at[t], row=rw(z - 1, k))

    def ring(t, carry):
        zz = zm(z + 4 - t)
        send_p(zz).wait_recv()
        part = chunk(zz, k) + precv[zz].astype(F32)

        @pl.when(t == 0)
        def _():
            usend[t] = part.astype(BF16)

        @pl.when(t > 0)
        def _():
            send_u(t - 1).wait_recv()
            usend[t] = (part + urecv[t - 1].astype(F32)).astype(BF16)

        send_u(t).start()

        @pl.when(t < 3)
        def _():
            zd = zm(z + 5 + t)
            send_p(zd).wait_recv()
            part_d = chunk(zd, k) + precv[zd].astype(F32)

            @pl.when(t == 0)
            def _():
                dsend[t] = part_d.astype(BF16)

            @pl.when(t > 0)
            def _():
                send_d(t - 1).wait_recv()
                dsend[t] = (part_d + drecv[t - 1].astype(F32)).astype(BF16)

            send_d(t).start()

        @pl.when(t == 1)
        def _():
            for j in range(1, NY):
                part_w = wg.at[x, ym(j)]
                rcopy(part_w, part_w, wy_s.at[j], wy_r.at[ym(j)], col=me_c).wait_recv()
            for j in range(1, NX):
                send_wx(j).start()

        return carry

    lax.fori_loop(0, 4, ring, 0)
    send_p(z).wait_recv()

    for j in range(1, NX):
        part_w = wg.at[xm(j)]
        rcopy(part_w, part_w, wx_s.at[j], wx_r.at[xm(j)], col=me_c).wait_recv()
    g_ws[...] = wg[0:2].reshape(256, 256) * scale
    g_wn[...] = wg[2:4].reshape(256, 256) * scale

    for u in range(4):
        ag_up(emb, me_r, u).wait_send()
        send_u(u).wait_send()
    for u in range(3):
        ag_down(emb, me_r, u).wait_send()
        send_d(u).wait_send()
    send_wp().wait_send()

    def drain_z(j, carry):
        ag_partner(emb, j * 2).wait_send()
        send_p(j).wait_send()
        return carry

    lax.fori_loop(0, NZ, drain_z, 0)

    def drain_wz(j, carry):
        send_wz(j).wait_send()
        return carry

    lax.fori_loop(1, NZ, drain_wz, 0)

    def drain_xy(j, carry):
        for copy in (
            send_a(j), send_b(j), send_a2(j), send_b2(j), send_dx(j), send_dy(j), full_x(j), full_y(j),
            send_w1(j), send_w2(j), send_wy(j), send_wx(j),
        ):
            copy.wait_send()
        for i in range(1, 4):
            half_a(j, i).wait_send()
            half_b(j, i).wait_send()
        return carry

    lax.fori_loop(1, 4, drain_xy, 0)

    send_u(3).wait_recv()
    send_d(2).wait_recv()
    grad_source[...] = (
        chunk(z, k) + precv[z].astype(F32) + urecv[3].astype(F32) + drecv[2].astype(F32)
    ).astype(BF16)


def body(
    source_emb, self_feat, w_self, w_neigh, bias, cotangent, tile_dst, tile_src, tile_live, tile_counts
):
    counts = tile_counts.reshape(SLOTS, 128, 128)
    slot = jnp.arange(SLOTS, dtype=jnp.int32)
    used = slot < tile_live.reshape(())
    dst = tile_dst.reshape(SLOTS)
    dkey = jnp.where(used, dst, -1)
    key = jnp.where(used, dst * NB + tile_src.reshape(SLOTS), -1)
    places = jnp.arange(NB * NB, dtype=jnp.int32)
    sel = ZERO_SLOT + jnp.sum(
        jnp.where(places[:, None] == key[None, :], slot[None, :] - ZERO_SLOT, 0), axis=1
    )
    scale = 1.0 / math.sqrt(self_feat.shape[0] * lax.axis_size("row") * lax.axis_size("col"))
    vm = pl.BlockSpec(memory_space=pltpu.VMEM)
    dma = pltpu.SemaphoreType.DMA
    v = pltpu.VMEM
    outs = pl.pallas_call(
        functools.partial(kernel, scale),
        out_shape=(
            jax.ShapeDtypeStruct((256, 256), BF16),
            jax.ShapeDtypeStruct((256, 256), BF16),
            jax.ShapeDtypeStruct((256, 256), BF16),
            jax.ShapeDtypeStruct((256, 256), F32),
            jax.ShapeDtypeStruct((256, 256), F32),
            jax.ShapeDtypeStruct((1, 256), F32),
        ),
        in_specs=[pl.BlockSpec(memory_space=pltpu.SMEM)] + [vm] * 7 + [pl.BlockSpec(memory_space=pl.ANY)],
        out_specs=(vm,) * 6,
        scratch_shapes=[
            v((SLOTS, 128, 128), jnp.int32),
            v((SLOTS + 1, 128, 128), BF16),
            v((SLOTS + 1, 128, 128), BF16),
            v((4096, 256), F32),
            v((16, 256, 256), BF16),
            v((NX, NY, 256, 128), BF16),
            v((NY, NX, 256, 128), BF16),
            v((NX, NY, 256, 128), BF16),
            v((NY, NX, 256, 128), BF16),
            v((NY, 256, 128), BF16),
            v((NX, 256, 128), BF16),
            v((NY, 256, 128), BF16),
            v((NX, 256, 128), BF16),
            v((256, 256), F32),
            v((SLOTS, 128), F32),
            v((NX, NY, 8, 128), F32),
            v((NX, NY, 8, 128), F32),
            v((NY, 8, 128), F32),
            v((NY, 8, 128), F32),
            v((256, 256), BF16),
            v((256, 256), BF16),
            v((16, 256, 256), BF16),
            v((NX, 144, 256), BF16),
            v((NX, 144, 256), BF16),
            v((NY, 40, 256), F32),
            v((NY, 40, 256), F32),
            v((40, 256), F32),
            v((40, 256), F32),
            v((NZ, 40, 256), F32),
            v((NX, NY, 32, 256), F32),
            v((NZ, 256, 256), BF16),
            v((NZ, 256, 256), BF16),
            v((4, 256, 256), BF16),
            v((4, 256, 256), BF16),
            v((3, 256, 256), BF16),
            v((3, 256, 256), BF16),
            dma((16,)),
            dma((16,)),
            dma((4,)),
            dma((3,)),
            dma((NZ,)),
            dma((4,)), dma((4,)),
            dma((4,)), dma((4,)),
            dma((4,)), dma((4,)),
            dma((4,)), dma((4,)),
            dma((4,)), dma((4,)),
            dma((4,)), dma((4,)),
            dma((7,)), dma((16,)),
            dma((16,)), dma((16,)),
            dma((16,)), dma((16,)),
            dma((4,)), dma((4,)),
            dma((4,)), dma((4,)),
            dma, dma,
            dma((NZ,)), dma((NZ,)),
            dma((4,)), dma((4,)),
            dma((4,)), dma((4,)),
            dma((NZ,)), dma((NZ,)),
            dma((4,)), dma((4,)),
            dma((3,)), dma((3,)),
        ],
        compiler_params=pltpu.CompilerParams(
            collective_id=0, has_side_effects=True, vmem_limit_bytes=56 * 1024 * 1024
        ),
    )(
        sel, dkey.reshape(1, SLOTS), source_emb, self_feat, w_self, w_neigh, bias.reshape(1, -1), cotangent, counts
    )
    layer_out, grad_self, grad_source, g_ws, g_wn, g_b = outs
    return layer_out, grad_self, grad_source, g_ws, g_wn, g_b.reshape(-1)


def solution(mesh):
    in_specs = (
        P(("col", "row"), None),
        P(("row", "col"), None),
        P(),
        P(),
        P(),
        P(("row", "col"), None),
        P("row", "col", None),
        P("row", "col", None),
        P("row", "col"),
        P("row", "col", None, None, None),
    )
    out_specs = (
        P(("row", "col"), None),
        P(("row", "col"), None),
        P(("col", "row"), None),
        P(),
        P(),
        P(),
    )
    return jax.shard_map(body, mesh=mesh, in_specs=in_specs, out_specs=out_specs, check_vma=False)
```

time: 580 us -> 120 us (0.21)
  the two profiles are of different devices: /device:TPU:1 before, /device:TPU:2 now
where the time goes in v1:
time: 120 us
  Pallas kernels  107 us (89%)
  local copies, waits for them, and re-layouts  9.23 us (8%)
  other arithmetic  2.66 us (2%)
  between operations  1.29 us (1%)
    pallas_call x1, Pallas kernels, body(): pl.pallas_call(functools.partial(kernel, scale), out_shape=(jax.ShapeDtyp...  107 us
    unnamed x6, local copies, waits for them, and re-layouts  9.23 us

profile of v1, /device:TPU:2, one launch (start us, length us, event | category | flops | bytes accessed | tf_op | source)
XLA Modules:
  0.0 119.8 jit_solution(9617763069311078613)
XLA Ops:
  1.3 1.2 compare_select_fusion.dkey
  2.4 0.7 compare_select_fusion.1
  3.1 0.2 select_reduce_fusion
  3.3 0.6 broadcast_add_fusion.sel
  3.9 106.6 %shard_map.145 = (bf16[256,256]{1,0:T(8,128)(2,1)}, bf16[256,256]{1,0:T(8,128)(2,1)}, bf16[256,256]{1,0:T(8,128)(2,1)}, f32[256,256]{1,0:T(8,128)}, f32[256,256]{1,0:T(8,128)}, /*index=5*/f32[1,256]{1,0:T(1,128)}) custom-call(s32[1024]{0:T(1024)} %broadcast_add_fusion.sel, s32[1,128]{1,0:T(1,128)} %compare_select_fusion.dkey, bf16[256,256]{1,0:T(8,128)(2,1)} %emb.1, ...), custom_call_target="tpu_custom_call" | custom-call | tf_op jit(solution)/shard_map/pallas_call | solution.py:627
  110.6 1.6 %copy.23 = bf16[256,256]{1,0:T(8,128)(2,1)} copy(bf16[256,256]{1,0:T(8,128)(2,1)} %get-tuple-element.26) | data formatting | bytes 262144
  112.1 1.6 %copy.24 = bf16[256,256]{1,0:T(8,128)(2,1)} copy(bf16[256,256]{1,0:T(8,128)(2,1)} %get-tuple-element.27) | data formatting | bytes 262144
  113.7 1.6 %copy.25 = bf16[256,256]{1,0:T(8,128)(2,1)} copy(bf16[256,256]{1,0:T(8,128)(2,1)} %get-tuple-element.28) | data formatting | bytes 262144
  115.3 1.7 %copy.26 = f32[256,256]{1,0:T(8,128)} copy(f32[256,256]{1,0:T(8,128)} %get-tuple-element.29) | data formatting | bytes 524288
  116.9 1.7 %copy.27 = f32[256,256]{1,0:T(8,128)} copy(f32[256,256]{1,0:T(8,128)} %get-tuple-element.30) | data formatting | bytes 524288
  118.6 1.2 copy.28

commit v2 on v1

v2 whole, which is shorter than its diff:
```python
import functools
import math

import jax
import jax.numpy as jnp
from jax import lax
from jax.experimental import pallas as pl
from jax.experimental.pallas import tpu as pltpu
from jax.sharding import PartitionSpec as P

F32, BF16 = jnp.float32, jnp.bfloat16
MESH = pl.DeviceIdType.MESH
NZ, NX, NY = 8, 4, 4
NB = 32
SLOTS = 128
ZERO_SLOT = SLOTS


def rcopy(src, dst, ssem, rsem, **where):
    return pltpu.make_async_remote_copy(
        src_ref=src, dst_ref=dst, send_sem=ssem, recv_sem=rsem, device_id=where, device_id_type=MESH
    )


def kernel(
    scale,
    dst_at, src_at, live_at, dst_ids, live, emb, feat, w_self, w_neigh, bias, cot, counts,
    layer_out, grad_self, grad_source, g_ws, g_wn, g_b,
    sel, selv, stage, cnt, cnt_t, acc, tab, sa, sb, ra, rb, s2a, s2b, r2a, r2b, nsum, rsum, dg0, dg1, dg2,
    dg3, agg, gpre, dtab, gwb, gwr, w1s, w1r, wz, x1s, x1r, gfin, psend, precv, esend, e3, e4, f1, f2,
    csem, selsem, ag_r, ag_s, ag_sp, sa_s, sa_r, sb_s, sb_r, s2a_s, s2a_r, s2b_s, s2b_r,
    dgx_s, dgx_r, dgy_s, dgy_r, df_s, df_r, da_s, da_r, db_s, db_r,
    w0_s, w0_r, w1_s, w1_r, w2_s, w2_r, x1_s, x1_r, x2_s, x2_r, pf_s, pf_r,
    p_s, p_r, e3_s, e3_r, e4_s, e4_r, f1_s, f1_r, f2_s, f2_r,
):
    me_r, me_c = lax.axis_index("row"), lax.axis_index("col")
    z, k = me_r // 2, me_r % 2
    x, y = me_c // NY, me_c % NY
    kp = 1 - k

    def zm(v):
        return (v + 2 * NZ) % NZ

    def rw(zz, kk):
        return zm(zz) * 2 + kk

    def xm(j):
        return (x + j) % NX

    def ym(j):
        return (y + j) % NY

    def cl(xx, yy):
        return xx * NY + yy

    partner = rw(z, kp)

    def count_copy(i):
        part = pl.ds(i * 8, 8)
        return pltpu.make_async_copy(counts.at[part], stage.at[part], csem.at[i])

    def start_counts(i, carry):
        count_copy(i).start()
        return carry


    barrier = pltpu.get_barrier_semaphore()

    def greet_z(j, carry):
        pl.semaphore_signal(barrier, inc=1, device_id={"row": rw(z + j, k)}, device_id_type=MESH)
        return carry

    def greet_c(j, carry):
        pl.semaphore_signal(barrier, inc=1, device_id={"col": (me_c + j) % 16}, device_id_type=MESH)
        return carry

    pl.semaphore_signal(barrier, inc=1, device_id={"row": partner}, device_id_type=MESH)
    lax.fori_loop(1, NZ, greet_z, 0)
    lax.fori_loop(1, NX * NY, greet_c, 0)

    line = lax.broadcasted_iota(jnp.int32, (128, 128), 0)
    lane = lax.broadcasted_iota(jnp.int32, (128, 128), 1)
    used = lane < live[...]
    nt = (((1,), (1,)), ((), ()))
    tn = (((0,), (0,)), ((), ()))
    place = line[0:NB] * NB + lane[0:NB]
    in_use = lane[0:NB] < NB
    place = jnp.where(in_use, place, -2)

    def put_slot(i, table):
        for u in range(8):
            s = i * 8 + u
            key = jnp.where(s < live_at[0, 0], dst_at[0, s] * NB + src_at[0, s], -1)
            table = jnp.where(place == key, s, table)
        return table

    selv[...] = lax.fori_loop(
        0, SLOTS // 8, put_slot, jnp.full((NB, 128), ZERO_SLOT, jnp.int32)
    )
    sel_copy = pltpu.make_async_copy(selv, sel, selsem)
    sel_copy.start()
    sel_copy.wait()

    pl.semaphore_wait(barrier, 1 + (NZ - 1) + (NX * NY - 1))

    def shard(r, h):
        return tab.at[r, h]

    def own(h):
        return emb.at[pl.ds(pl.multiple_of(h * 128, 128), 128), :]

    def ag_send(src, r, h, i, dz):
        return rcopy(src, shard(r, h), ag_s.at[i, h], ag_r.at[r, h], row=rw(z + dz, k))

    def ag_partner(src, r, h):
        return rcopy(src, shard(r, h), ag_sp.at[r // 2, h], ag_r.at[r, h], row=partner)

    def ag_wait(r, h):
        rcopy(shard(r, h), shard(r, h), ag_sp.at[r // 2, h], ag_r.at[r, h], row=partner).wait_recv()

    for h in range(2):
        ag_send(own(h), me_r, h, 0, 2).start()
        ag_send(own(h), me_r, h, 1, -2).start()
        ag_send(own(h), me_r, h, 2, 1).start()
        ag_send(own(h), me_r, h, 3, -1).start()
    for h in range(2):
        ag_partner(own(h), me_r, h).start()
    lax.fori_loop(0, 16, start_counts, 0)
    tab[me_r, 0] = emb[0:128]
    tab[me_r, 1] = emb[128:256]
    cnt[ZERO_SLOT] = jnp.zeros((128, 128), BF16)
    cnt_t[ZERO_SLOT] = jnp.zeros((128, 128), BF16)

    def zero_acc(i, carry):
        acc[pl.ds(pl.multiple_of(i * 256, 256), 256), :] = jnp.zeros((256, 256), F32)
        return carry

    lax.fori_loop(0, 16, zero_acc, 0)

    def convert(i, carry):
        count_copy(i).wait()
        part = pl.ds(i * 8, 8)
        cnt[part] = stage[part].astype(F32).astype(BF16)
        return carry

    lax.fori_loop(0, 16, convert, 0)

    def spmm_block(tiles, pick, rhs, b, n, shards):
        rows = []
        for i in range(n):
            parts = []
            for s in shards:
                parts += [tiles[pick(b * n + i, 2 * s)], tiles[pick(b * n + i, 2 * s + 1)]]
            rows.append(jnp.concatenate(parts, axis=1))
        lhs = jnp.concatenate(rows, axis=0)
        r = pl.ds(pl.multiple_of(b * n * 128, n * 128), n * 128)
        acc[r, :] += jnp.dot(
            lhs, jnp.concatenate([rhs(s) for s in shards], axis=0), preferred_element_type=F32
        )

    def spmm(tiles, pick, rhs, shards):
        def block(b, carry):
            spmm_block(tiles, pick, rhs, b, 16, shards)
            return carry

        lax.fori_loop(0, NB // 16, block, 0)

    def source_rows(s):
        return tab[s].reshape(256, 256)

    def grad_rows(s):
        return jnp.concatenate([dtab[s, 0], dtab[s, 1]], axis=1)

    def fwd_pick(d, s):
        return sel[d, s]

    def bwd_pick(s, d):
        return sel[d, s]

    def transpose(i, carry):
        for u in range(4):
            t = cnt[i * 4 + u].T
            cnt_t[i * 4 + u] = t
            rsum[pl.ds(i * 4 + u, 1), :] = jnp.sum(t.astype(F32), axis=0, keepdims=True)
        return carry

    def ag_step(t, carry):
        h = t % 2

        def take(r):
            ag_wait(r, h)
            ag_partner(shard(r, h), r, h).start()

        @pl.when(t < 2)
        def _():
            up, down = rw(z - 2, k), rw(z + 2, k)
            ag_wait(up, h)
            ag_send(shard(up, h), up, h, 4, 1).start()

            @pl.when(h == 0)
            def _():
                ag_send(shard(up, h), up, h, 6, 2).start()

            ag_wait(down, h)
            ag_send(shard(down, h), down, h, 5, -1).start()

            @pl.when(h == 1)
            def _():
                ag_send(shard(down, h), down, h, 6, -2).start()

            ag_partner(shard(up, h), up, h).start()
            ag_partner(shard(down, h), down, h).start()
            take(rw(z - 1, k))
            take(rw(z + 1, k))

        @pl.when(t >= 2)
        def _():
            take(rw(z - 3, k))
            take(rw(z + 3, k))
            take(rw(z + 4, k))

        lax.fori_loop(t * 8, t * 8 + 8, transpose, 0)

        @pl.when(t == 0)
        def _():
            for h in range(2):
                ag_wait(partner, h)

        @pl.when(t == 2)
        def _():
            for h in range(2):
                ag_wait(rw(z - 1, kp), h)
                ag_wait(rw(z + 1, kp), h)

        dz = (t + 1) // 2
        s0 = rw(z - dz, (k + (t // 2) * (3 - t)) % 2)
        s1 = rw(z + dz, (k + (t + 1) % 2) % 2)
        spmm(cnt, fwd_pick, source_rows, (s0, s1))
        return carry

    lax.fori_loop(0, 4, ag_step, 0)

    hot = ((line // 8) * 2 + line % 8 == dst_ids[...]) & (line % 8 < 2) & used
    hot = jnp.where(hot, 1.0, 0.0).astype(BF16)
    part_a = jnp.minimum(rsum[...], 256.0)
    part_b = rsum[...] - part_a
    part_deg = jnp.dot(hot, part_a.astype(BF16), preferred_element_type=F32) + jnp.dot(
        hot, part_b.astype(BF16), preferred_element_type=F32
    )
    dg0[...] = part_deg.reshape(NX, NY, 8, 128)

    def send_dx(j):
        return rcopy(dg0.at[xm(j)], dg1.at[x], dgx_s.at[j], dgx_r.at[x], col=cl(xm(j), y))

    def send_dy(j):
        return rcopy(dg2.at[ym(j)], dg3.at[y], dgy_s.at[j], dgy_r.at[y], col=cl(x, ym(j)))

    for j in range(1, NX):
        send_dx(j).start()
    dg1[x] = dg0[x]

    for h in range(2):
        for dz in (2, 3):
            ag_wait(rw(z - dz, kp), h)
            ag_wait(rw(z + dz, kp), h)
        ag_wait(rw(z - 4, kp), h)

    def send_a(j):
        return rcopy(sa.at[xm(j)], ra.at[x], sa_s.at[j], sa_r.at[x], col=cl(xm(j), y))

    def send_b(jy, xx):
        return rcopy(
            sb.at[ym(jy), xx], rb.at[y, xx], sb_s.at[jy, xx], sb_r.at[y, xx], col=cl(x, ym(jy))
        )

    def emit(jx, carry):
        xx = xm(jx)

        def rest(i, carry):
            shards = ()
            for g in (2 * i, 2 * i + 1):
                dz = 2 + (g + 1) // 2
                shards += (
                    rw(z - dz, (k + (g + 1) % 2) % 2),
                    rw(z + dz, (k + (g + 1) % 2 + g // 3) % 2),
                )
            spmm_block(cnt, fwd_pick, source_rows, xx, 8, shards)
            return carry

        lax.fori_loop(0, 2, rest, 0)

        def put(yy, carry):
            r = pl.ds(pl.multiple_of(cl(xx, yy) * 256, 256), 256)
            sa[xx, yy] = acc[r, 0:128].astype(BF16)
            sb[yy, xx] = acc[r, 128:256].astype(BF16)
            return carry

        lax.fori_loop(0, NY, put, 0)

        @pl.when(jx < 4)
        def _():
            send_a(jx).start()

        for j in range(1, NY):
            send_b(j, xx).start()
        return carry

    lax.fori_loop(1, 5, emit, 0)
    lax.fori_loop(0, 16, zero_acc, 0)
    for j in range(1, NX):
        rcopy(dg1.at[xm(j)], dg1.at[xm(j)], dgx_s.at[j], dgx_r.at[xm(j)], col=me_c).wait_recv()
    dg2[...] = dg1[0] + dg1[1] + dg1[2] + dg1[3]
    for j in range(1, NY):
        send_dy(j).start()

    def send_a2(j):
        return rcopy(s2a.at[ym(j)], r2a.at[y], s2a_s.at[j], s2a_r.at[y], col=cl(x, ym(j)))

    def send_b2(j):
        return rcopy(s2b.at[xm(j)], r2b.at[x], s2b_s.at[j], s2b_r.at[x], col=cl(xm(j), y))

    def sum_a(yy):
        return (
            sa[x, yy].astype(F32)
            + ra[xm(1), yy].astype(F32)
            + ra[xm(2), yy].astype(F32)
            + ra[xm(3), yy].astype(F32)
        )

    def sum_b(xx):
        return (
            sb[y, xx].astype(F32)
            + rb[ym(1), xx].astype(F32)
            + rb[ym(2), xx].astype(F32)
            + rb[ym(3), xx].astype(F32)
        )

    def wait_b(xx):
        for j in range(1, NY):
            part = rb.at[ym(j), xx]
            rcopy(part, part, sb_s.at[j, xx], sb_r.at[ym(j), xx], col=me_c).wait_recv()

    def stage_b2(j, carry):
        wait_b(xm(j))
        s2b[xm(j)] = sum_b(xm(j)).astype(BF16)
        send_b2(j).start()
        return carry

    lax.fori_loop(1, NX, stage_b2, 0)
    for j in range(1, NX):
        rcopy(ra.at[xm(j)], ra.at[xm(j)], sa_s.at[j], sa_r.at[xm(j)], col=me_c).wait_recv()

    def stage_a2(j, carry):
        s2a[ym(j)] = sum_a(ym(j)).astype(BF16)
        send_a2(j).start()
        return carry

    lax.fori_loop(1, NY, stage_a2, 0)
    wait_b(x)
    nsum[:, 0:128] = sum_a(y)
    nsum[:, 128:256] = sum_b(x)

    dg3[y] = dg2[y]
    for j in range(1, NY):
        rcopy(dg3.at[ym(j)], dg3.at[ym(j)], dgy_s.at[j], dgy_r.at[ym(j)], col=me_c).wait_recv()
    degree = dg3[0] + dg3[1] + dg3[2] + dg3[3]
    inv_lane = 1.0 / jnp.sqrt(degree + 1.0)
    eye = line == lane
    inv_col = jnp.concatenate(
        [
            jnp.sum(jnp.where(eye, inv_lane[b : b + 1, :], 0.0), axis=1, keepdims=True)
            for b in range(2)
        ],
        axis=0,
    )

    for j in range(1, NY):
        rcopy(r2a.at[ym(j)], r2a.at[ym(j)], s2a_s.at[j], s2a_r.at[ym(j)], col=me_c).wait_recv()
    nsum[:, 0:128] += (
        r2a[ym(1)].astype(F32) + r2a[ym(2)].astype(F32) + r2a[ym(3)].astype(F32)
    )
    for j in range(1, NX):
        rcopy(r2b.at[xm(j)], r2b.at[xm(j)], s2b_s.at[j], s2b_r.at[xm(j)], col=me_c).wait_recv()
    nsum[:, 128:256] += (
        r2b[xm(1)].astype(F32) + r2b[xm(2)].astype(F32) + r2b[xm(3)].astype(F32)
    )

    agg[...] = (nsum[...] * inv_col).astype(BF16)
    pre = (
        jnp.dot(feat[...], w_self[...], preferred_element_type=F32)
        + jnp.dot(agg[...], w_neigh[...], preferred_element_type=F32)
        + bias[...]
    )
    sig = jax.nn.sigmoid(pre)
    layer_out[...] = (pre * sig).astype(BF16)
    gpre[...] = (cot[...].astype(F32) * sig * (1.0 + pre * (1.0 - sig))).astype(BF16)
    gsum = (
        lax.dot_general(gpre[...], w_neigh[...], nt, preferred_element_type=F32) * inv_col
    ).astype(BF16)
    dtab[me_c, 0] = gsum[:, 0:128]
    dtab[me_c, 1] = gsum[:, 128:256]

    def full_x(j):
        return rcopy(dtab.at[me_c], dtab.at[me_c], df_s.at[j], df_r.at[me_c], col=cl(xm(j), y))

    def full_y(j):
        return rcopy(dtab.at[me_c], dtab.at[me_c], df_s.at[3 + j], df_r.at[me_c], col=cl(x, ym(j)))

    def half_a(jx, jy):
        part = dtab.at[cl(xm(jx), y), 0]
        return rcopy(
            part, part, da_s.at[jx * 4 + jy], da_r.at[cl(xm(jx), y)], col=cl(x, ym(jy))
        )

    def half_b(jx, jy):
        part = dtab.at[cl(x, ym(jy)), 1]
        return rcopy(
            part, part, db_s.at[jx * 4 + jy], db_r.at[cl(x, ym(jy))], col=cl(xm(jx), y)
        )

    def start_full(j, carry):
        full_x(j).start()
        full_y(j).start()
        return carry

    lax.fori_loop(1, 4, start_full, 0)

    grad_self[...] = lax.dot_general(
        gpre[...], w_self[...], nt, preferred_element_type=F32
    ).astype(BF16)
    gwb[0, 0:256, :] = lax.dot_general(feat[...], gpre[...], tn, preferred_element_type=F32)
    gwb[1, 0:256, :] = lax.dot_general(agg[...], gpre[...], tn, preferred_element_type=F32)
    gb = jnp.broadcast_to(jnp.sum(gpre[...].astype(F32), axis=0, keepdims=True), (8, 256))
    gwb[0, 256:264, :] = gb
    gwb[1, 256:264, :] = gb

    def send_w0():
        return rcopy(gwb.at[kp], gwr, w0_s, w0_r, row=partner)

    def send_w1(j):
        zz = zm(z + j)
        return rcopy(w1s.at[zz], w1r.at[z], w1_s.at[j], w1_r.at[z], row=rw(zz, k))

    def send_w2(j):
        return rcopy(wz.at[z], wz.at[z], w2_s.at[j], w2_r.at[z], row=rw(z + j, k))

    def send_x1(j):
        c = (me_c + j) % 16
        return rcopy(x1s.at[c], x1r.at[me_c], x1_s.at[j], x1_r.at[me_c], col=c)

    def send_x2(j):
        part = gfin.at[k, me_c]
        return rcopy(part, part, x2_s.at[j], x2_r.at[me_c], col=(me_c + j) % 16)

    def send_pf():
        return rcopy(gfin.at[k], gfin.at[k], pf_s, pf_r, row=partner)

    send_w0().start()

    def take_x(jx):
        c = cl(xm(jx), y)
        rcopy(dtab.at[c], dtab.at[c], df_s.at[jx], df_r.at[c], col=me_c).wait_recv()

        def go(jy, carry):
            half_a(jx, jy).start()
            return carry

        lax.fori_loop(1, 4, go, 0)

    def take_y(jy):
        c = cl(x, ym(jy))
        rcopy(dtab.at[c], dtab.at[c], df_s.at[jy], df_r.at[c], col=me_c).wait_recv()

        def go(jx, carry):
            half_b(jx, jy).start()
            return carry

        lax.fori_loop(1, 4, go, 0)

    def take_rest(c):
        part = dtab.at[c, 0]
        rcopy(part, part, da_s.at[0], da_r.at[c], col=me_c).wait_recv()
        part = dtab.at[c, 1]
        rcopy(part, part, db_s.at[0], db_r.at[c], col=me_c).wait_recv()

    take_x(1)
    take_y(1)
    take_x(3)
    take_y(3)
    send_w0().wait_recv()
    gwb[k] = gwb[k] + gwr[...]

    def split_z(j, carry):
        w1s[j, 0:32, :] = gwb[k, pl.ds(pl.multiple_of(j * 32, 32), 32), :].astype(BF16)
        w1s[j, 32:48, :] = jnp.concatenate([gwb[k, 256:264, :]] * 2, axis=0).astype(BF16)
        return carry

    lax.fori_loop(0, NZ, split_z, 0)
    for j in range(1, NZ):
        send_w1(j).start()
    w1r[z] = w1s[z]

    def order(q):
        m = q - 7
        dx = jnp.where(q < 4, q, jnp.where(q < 7, 0, 1 + m // 3))
        dy = jnp.where(q < 4, 0, jnp.where(q < 7, q - 3, 1 + m % 3))
        return cl(xm(dx), ym(dy))

    def bwd_step(g, carry):
        @pl.when(g == 1)
        def _():
            take_x(2)
            take_y(2)

        @pl.when(g == 3)
        def _():
            for j in range(1, NZ):
                zz = zm(z + j)
                rcopy(w1r.at[zz], w1r.at[zz], w1_s.at[j], w1_r.at[zz], row=me_r).wait_recv()
            tot = w1r[0].astype(F32)
            for j in range(1, NZ):
                tot = tot + w1r[j].astype(F32)
            wz[z] = tot[0:32]
            gwb[k, 256:264, :] = tot[32:40]
            for j in range(1, NZ):
                send_w2(j).start()

        @pl.when(g > 3)
        def _():
            take_rest(order(2 * g))

        @pl.when(g > 2)
        def _():
            take_rest(order(2 * g + 1))

        spmm(cnt_t, bwd_pick, grad_rows, (order(2 * g), order(2 * g + 1)))
        return carry

    lax.fori_loop(0, 6, bwd_step, 0)
    last = tuple(order(q) for q in range(12, 16))
    for c in last:
        take_rest(c)

    def chunk(zz, kk):
        return acc[pl.ds(pl.multiple_of(rw(zz, kk) * 256, 256), 256), :]

    def send_p(zz):
        return rcopy(psend.at[zz], precv.at[zz], p_s.at[zz], p_r.at[zz], row=partner)

    def put_p(zz):
        psend[zz] = chunk(zz, kp).astype(BF16)
        send_p(zz).start()

    def finish(zz):
        spmm_block(cnt_t, bwd_pick, grad_rows, zz, 4, last)
        put_p(zz)

    def rows_of(h):
        return pl.ds(pl.multiple_of(h * 128, 128), 128)

    def own_part(zz, h):
        r = pl.ds(pl.multiple_of(rw(zz, k) * 256 + h * 128, 128), 128)
        return acc[r, :] + precv[zz, rows_of(h), :].astype(F32)

    def send_e3(i, h):
        return rcopy(
            esend.at[i, h], e3.at[i, h], e3_s.at[i, h], e3_r.at[i, h], row=rw(z + 1 - 2 * i, k)
        )

    def send_e4(i):
        return rcopy(esend.at[2, i], e4.at[i], e4_s.at[i], e4_r.at[i], row=rw(z + 2 - 4 * i, k))

    def send_f1(i, h):
        return rcopy(
            esend.at[3 + i, h], f1.at[i, h], f1_s.at[i, h], f1_r.at[i, h], row=rw(z + 1 - 2 * i, k)
        )

    def send_f2(i, h):
        return rcopy(
            esend.at[5 + i, h], f2.at[i, h], f2_s.at[i, h], f2_r.at[i, h], row=rw(z + 2 - 4 * i, k)
        )

    def finish_at(j, carry):
        dz = (3 + 2 * j) * (j < 2) + 4 * (j == 2) + (2 + 4 * (j - 3)) * ((j > 2) & (j < 5)) + (
            1 + 6 * (j - 5)
        ) * ((j > 4) & (j < 7))
        finish(zm(z + dz))
        return carry

    lax.fori_loop(0, 3, finish_at, 0)

    def first_hop(i, carry):
        zz = zm(z + 3 + 2 * i)
        send_p(zz).wait_recv()
        for h in range(2):
            esend[i, h] = own_part(zz, h).astype(BF16)
            send_e3(i, h).start()
        return carry

    lax.fori_loop(0, 2, first_hop, 0)
    send_p(zm(z + 4)).wait_recv()
    for h in range(2):
        esend[2, h] = own_part(zm(z + 4), h).astype(BF16)
        send_e4(h).start()

    lax.fori_loop(3, 8, finish_at, 0)

    def to_next(i, carry):
        zz = zm(z + 1 + 6 * i)
        send_p(zz).wait_recv()
        for h in range(2):
            esend[3 + i, h] = own_part(zz, h).astype(BF16)
            send_f1(i, h).start()
        return carry

    lax.fori_loop(0, 2, to_next, 0)

    for j in range(1, NZ):
        zz = zm(z + j)
        rcopy(wz.at[zz], wz.at[zz], w2_s.at[j], w2_r.at[zz], row=me_r).wait_recv()

    def split_c(i, carry):
        for u in range(2):
            x1s[2 * i + u, 0:16, :] = wz[i, u * 16 : u * 16 + 16, :]
            x1s[2 * i + u, 16:24, :] = gwb[k, 256:264, :]
        return carry

    lax.fori_loop(0, NZ, split_c, 0)
    x1r[me_c] = x1s[me_c]

    def start_x1(j, carry):
        send_x1(j).start()
        return carry

    lax.fori_loop(1, NX * NY, start_x1, 0)

    def to_second(i, carry):
        zz = zm(z + 2 + 4 * i)
        send_p(zz).wait_recv()
        for h in range(2):
            send_e3(i, h).wait_recv()

            @pl.when(i == h)
            def _():
                send_e4(h).wait_recv()
                esend[5 + i, h] = (
                    own_part(zz, h) + e3[i, h].astype(F32) + e4[h].astype(F32)
                ).astype(BF16)

            @pl.when(i != h)
            def _():
                esend[5 + i, h] = (own_part(zz, h) + e3[i, h].astype(F32)).astype(BF16)

            send_f2(i, h).start()
        return carry

    lax.fori_loop(0, 2, to_second, 0)

    def wait_x1(j, carry):
        c = (me_c + j) % 16
        rcopy(x1r.at[c], x1r.at[c], x1_s.at[j], x1_r.at[c], col=me_c).wait_recv()
        return carry

    lax.fori_loop(1, NX * NY, wait_x1, 0)
    tot = x1r[0]
    for c in range(1, NX * NY):
        tot = tot + x1r[c]
    g_b[...] = tot[16:17] * scale
    gfin[k, me_c] = tot[0:16] * scale

    def start_x2(j, carry):
        send_x2(j).start()
        return carry

    lax.fori_loop(1, NX * NY, start_x2, 0)
    send_p(z).wait_recv()
    for h in range(2):
        for i in range(2):
            send_f1(i, h).wait_recv()
        nsum[h * 128 : h * 128 + 128, :] = (
            own_part(z, h) + f1[0, h].astype(F32) + f1[1, h].astype(F32)
        )

    def wait_x2(j, carry):
        c = (me_c + j) % 16
        part = gfin.at[k, c]
        rcopy(part, part, x2_s.at[j], x2_r.at[c], col=me_c).wait_recv()
        return carry

    lax.fori_loop(1, NX * NY, wait_x2, 0)
    send_pf().start()
    for h in range(2):
        for i in range(2):
            send_f2(i, h).wait_recv()
        grad_source[h * 128 : h * 128 + 128, :] = (
            nsum[h * 128 : h * 128 + 128, :] + f2[0, h].astype(F32) + f2[1, h].astype(F32)
        ).astype(BF16)
    rcopy(gfin.at[kp], gfin.at[kp], pf_s, pf_r, row=partner).wait_recv()
    g_ws[...] = gfin[0].reshape(256, 256)
    g_wn[...] = gfin[1].reshape(256, 256)

    def drain_h(h, carry):
        for i in range(7):
            ag_send(own(h), me_r, h, i, 1).wait_send()
        for j in range(NZ):
            ag_partner(own(h), j * 2, h).wait_send()
        for i in range(2):
            send_e3(i, h).wait_send()
            send_f1(i, h).wait_send()
            send_f2(i, h).wait_send()
        send_e4(h).wait_send()
        return carry

    lax.fori_loop(0, 2, drain_h, 0)
    send_w0().wait_send()
    send_pf().wait_send()
    send_p(0).wait_send()

    def drain_z(j, carry):
        send_p(j).wait_send()
        send_w1(j).wait_send()
        send_w2(j).wait_send()
        return carry

    lax.fori_loop(1, NZ, drain_z, 0)

    def drain_c(j, carry):
        send_x1(j).wait_send()
        send_x2(j).wait_send()
        return carry

    lax.fori_loop(1, NX * NY, drain_c, 0)

    def drain_xy(j, carry):
        for copy in (send_a(j), send_a2(j), send_b2(j), send_dx(j), send_dy(j), full_x(j), full_y(j)):
            copy.wait_send()
        for i in range(1, 4):
            half_a(j, i).wait_send()
            half_b(j, i).wait_send()
        for i in range(4):
            send_b(j, i).wait_send()
        return carry

    lax.fori_loop(1, 4, drain_xy, 0)


def hand_over(*refs):
    n = len(refs) // 2
    for i in range(n):
        refs[n + i][...] = refs[i][...]


def body(
    source_emb, self_feat, w_self, w_neigh, bias, cotangent, tile_dst, tile_src, tile_live, tile_counts
):
    counts = tile_counts.reshape(SLOTS, 128, 128)
    dst, src = tile_dst.reshape(1, SLOTS), tile_src.reshape(1, SLOTS)
    scale = 1.0 / math.sqrt(self_feat.shape[0] * lax.axis_size("row") * lax.axis_size("col"))
    vm = pl.BlockSpec(memory_space=pltpu.VMEM)
    dma = pltpu.SemaphoreType.DMA
    v = pltpu.VMEM
    outs = pl.pallas_call(
        functools.partial(kernel, scale),
        out_shape=(
            jax.ShapeDtypeStruct((256, 256), BF16),
            jax.ShapeDtypeStruct((256, 256), BF16),
            jax.ShapeDtypeStruct((256, 256), BF16),
            jax.ShapeDtypeStruct((256, 256), F32),
            jax.ShapeDtypeStruct((256, 256), F32),
            jax.ShapeDtypeStruct((1, 256), F32),
        ),
        in_specs=[pl.BlockSpec(memory_space=pltpu.SMEM)] * 3 + [vm] * 8 + [pl.BlockSpec(memory_space=pl.ANY)],
        out_specs=(vm,) * 6,
        scratch_shapes=[
            pltpu.SMEM((NB, 128), jnp.int32),
            v((NB, 128), jnp.int32),
            v((SLOTS, 128, 128), jnp.int32),
            v((SLOTS + 1, 128, 128), BF16),
            v((SLOTS + 1, 128, 128), BF16),
            v((4096, 256), F32),
            v((16, 2, 128, 256), BF16),
            v((NX, NY, 256, 128), BF16),
            v((NY, NX, 256, 128), BF16),
            v((NX, NY, 256, 128), BF16),
            v((NY, NX, 256, 128), BF16),
            v((NY, 256, 128), BF16),
            v((NX, 256, 128), BF16),
            v((NY, 256, 128), BF16),
            v((NX, 256, 128), BF16),
            v((256, 256), F32),
            v((SLOTS, 128), F32),
            v((NX, NY, 8, 128), F32),
            v((NX, NY, 8, 128), F32),
            v((NY, 8, 128), F32),
            v((NY, 8, 128), F32),
            v((256, 256), BF16),
            v((256, 256), BF16),
            v((16, 2, 256, 128), BF16),
            v((2, 264, 256), F32),
            v((264, 256), F32),
            v((NZ, 48, 256), BF16),
            v((NZ, 48, 256), BF16),
            v((NZ, 32, 256), F32),
            v((16, 24, 256), F32),
            v((16, 24, 256), F32),
            v((2, 16, 16, 256), F32),
            v((NZ, 256, 256), BF16),
            v((NZ, 256, 256), BF16),
            v((7, 2, 128, 256), BF16),
            v((2, 2, 128, 256), BF16),
            v((2, 128, 256), BF16),
            v((2, 2, 128, 256), BF16),
            v((2, 2, 128, 256), BF16),
            dma((16,)),
            dma,
            dma((16, 2)),
            dma((7, 2)),
            dma((NZ, 2)),
            dma((4,)), dma((4,)),
            dma((4, 4)), dma((4, 4)),
            dma((4,)), dma((4,)),
            dma((4,)), dma((4,)),
            dma((4,)), dma((4,)),
            dma((4,)), dma((4,)),
            dma((7,)), dma((16,)),
            dma((16,)), dma((16,)),
            dma((16,)), dma((16,)),
            dma, dma,
            dma((NZ,)), dma((NZ,)),
            dma((NZ,)), dma((NZ,)),
            dma((16,)), dma((16,)),
            dma((16,)), dma((16,)),
            dma, dma,
            dma((NZ,)), dma((NZ,)),
            dma((2, 2)), dma((2, 2)),
            dma((2,)), dma((2,)),
            dma((2, 2)), dma((2, 2)),
            dma((2, 2)), dma((2, 2)),
        ],
        compiler_params=pltpu.CompilerParams(
            collective_id=0, has_side_effects=True, vmem_limit_bytes=56 * 1024 * 1024
        ),
    )(
        dst, src, tile_live, dst, tile_live,
        source_emb, self_feat, w_self, w_neigh, bias.reshape(1, -1), cotangent, counts,
    )
    outs = pl.pallas_call(
        hand_over,
        out_shape=tuple(jax.ShapeDtypeStruct(o.shape, o.dtype) for o in outs),
        in_specs=[vm] * 6,
        out_specs=(vm,) * 6,
    )(*outs)
    layer_out, grad_self, grad_source, g_ws, g_wn, g_b = outs
    return layer_out, grad_self, grad_source, g_ws, g_wn, g_b.reshape(-1)


def solution(mesh):
    in_specs = (
        P(("col", "row"), None),
        P(("row", "col"), None),
        P(),
        P(),
        P(),
        P(("row", "col"), None),
        P("row", "col", None),
        P("row", "col", None),
        P("row", "col"),
        P("row", "col", None, None, None),
    )
    out_specs = (
        P(("row", "col"), None),
        P(("row", "col"), None),
        P(("col", "row"), None),
        P(),
        P(),
        P(),
    )
    return jax.shard_map(body, mesh=mesh, in_specs=in_specs, out_specs=out_specs, check_vma=False)
```

time: 120 us -> 103 us (0.86)
  the two profiles are of different devices: /device:TPU:2 before, /device:TPU:1 now
where the time goes in v2:
time: 103 us
  Pallas kernels  102 us (99%)
  between operations  1.29 us (1%)
    pallas_call x1, Pallas kernels, body(): pl.pallas_call(functools.partial(kernel, scale), out_shape=(jax.ShapeDtyp...  99.8 us
    pallas_call x1, Pallas kernels, body(): pl.pallas_call(hand_over, out_shape=tuple((jax.ShapeDtypeStruct(o.shape,...  2.14 us

profile of v2, /device:TPU:1, one launch (start us, length us, event | category | flops | bytes accessed | tf_op | source)
XLA Modules:
  0.0 103.3 jit_solution(16700343134108320248)
XLA Ops:
  1.3 99.8 %shard_map.145 = (bf16[256,256]{1,0:T(8,128)(2,1)}, bf16[256,256]{1,0:T(8,128)(2,1)}, bf16[256,256]{1,0:T(8,128)(2,1)}, f32[256,256]{1,0:T(8,128)}, f32[256,256]{1,0:T(8,128)}, /*index=5*/f32[1,256]{1,0:T(1,128)}) custom-call(s32[1,128]{1,0:T(1,128)} %bitcast.6, s32[1,128]{1,0:T(1,128)} %bitcast.9, s32[1,1]{1,0:T(1,128)S(6)} %copy.16.live_at.live, ...), custom_call_target="tpu_custom_call" | custom-call | tf_op jit(solution)/shard_map/pallas_call | solution.py:762
  101.1 2.1 %shard_map.146 = (bf16[256,256]{1,0:T(8,128)(2,1)}, bf16[256,256]{1,0:T(8,128)(2,1)}, bf16[256,256]{1,0:T(8,128)(2,1)}, f32[256,256]{1,0:T(8,128)}, f32[256,256]{1,0:T(8,128)}, /*index=5*/f32[1,256]{1,0:T(1,128)}) custom-call(bf16[256,256]{1,0:T(8,128)(2,1)} %get-tuple-element.18.refs_0_, bf16[256,256]{1,0:T(8,128)(2,1)} %get-tuple-element.19.refs_1_, ...), custom_call_target="tpu_custom_call" | custom-call | tf_op jit(solution)/shard_map/pallas_call | solution.py:847

commit v3 on v2

--- a/solution.py
+++ b/solution.py
@@ -31,7 +31,7 @@
     csem, selsem, ag_r, ag_s, ag_sp, sa_s, sa_r, sb_s, sb_r, s2a_s, s2a_r, s2b_s, s2b_r,
     dgx_s, dgx_r, dgy_s, dgy_r, df_s, df_r, da_s, da_r, db_s, db_r,
     w0_s, w0_r, w1_s, w1_r, w2_s, w2_r, x1_s, x1_r, x2_s, x2_r, pf_s, pf_r,
-    p_s, p_r, e3_s, e3_r, e4_s, e4_r, f1_s, f1_r, f2_s, f2_r,
+    p_s, p_r, e_s, e3_r, e4_r, f1_r, f2_r,
 ):
     me_r, me_c = lax.axis_index("row"), lax.axis_index("col")
     z, k = me_r // 2, me_r % 2
@@ -110,13 +110,13 @@
         return emb.at[pl.ds(pl.multiple_of(h * 128, 128), 128), :]
 
     def ag_send(src, r, h, i, dz):
-        return rcopy(src, shard(r, h), ag_s.at[i, h], ag_r.at[r, h], row=rw(z + dz, k))
+        return rcopy(src, shard(r, h), ag_s, ag_r.at[r, h], row=rw(z + dz, k))
 
     def ag_partner(src, r, h):
-        return rcopy(src, shard(r, h), ag_sp.at[r // 2, h], ag_r.at[r, h], row=partner)
+        return rcopy(src, shard(r, h), ag_sp, ag_r.at[r, h], row=partner)
 
     def ag_wait(r, h):
-        rcopy(shard(r, h), shard(r, h), ag_sp.at[r // 2, h], ag_r.at[r, h], row=partner).wait_recv()
+        rcopy(shard(r, h), shard(r, h), ag_sp, ag_r.at[r, h], row=partner).wait_recv()
 
     for h in range(2):
         ag_send(own(h), me_r, h, 0, 2).start()
@@ -250,10 +250,10 @@
     dg0[...] = part_deg.reshape(NX, NY, 8, 128)
 
     def send_dx(j):
-        return rcopy(dg0.at[xm(j)], dg1.at[x], dgx_s.at[j], dgx_r.at[x], col=cl(xm(j), y))
+        return rcopy(dg0.at[xm(j)], dg1.at[x], dgx_s, dgx_r, col=cl(xm(j), y))
 
     def send_dy(j):
-        return rcopy(dg2.at[ym(j)], dg3.at[y], dgy_s.at[j], dgy_r.at[y], col=cl(x, ym(j)))
+        return rcopy(dg2.at[ym(j)], dg3.at[y], dgy_s, dgy_r, col=cl(x, ym(j)))
 
     for j in range(1, NX):
         send_dx(j).start()
@@ -266,11 +266,11 @@
         ag_wait(rw(z - 4, kp), h)
 
     def send_a(j):
-        return rcopy(sa.at[xm(j)], ra.at[x], sa_s.at[j], sa_r.at[x], col=cl(xm(j), y))
+        return rcopy(sa.at[xm(j)], ra.at[x], sa_s, sa_r, col=cl(xm(j), y))
 
     def send_b(jy, xx):
         return rcopy(
-            sb.at[ym(jy), xx], rb.at[y, xx], sb_s.at[jy, xx], sb_r.at[y, xx], col=cl(x, ym(jy))
+            sb.at[ym(jy), xx], rb.at[y, xx], sb_s, sb_r.at[y, xx], col=cl(x, ym(jy))
         )
 
     def emit(jx, carry):
@@ -307,17 +307,16 @@
 
     lax.fori_loop(1, 5, emit, 0)
     lax.fori_loop(0, 16, zero_acc, 0)
-    for j in range(1, NX):
-        rcopy(dg1.at[xm(j)], dg1.at[xm(j)], dgx_s.at[j], dgx_r.at[xm(j)], col=me_c).wait_recv()
+    rcopy(dg1.at[0:3], dg1.at[0:3], dgx_s, dgx_r, row=partner).wait_recv()
     dg2[...] = dg1[0] + dg1[1] + dg1[2] + dg1[3]
     for j in range(1, NY):
         send_dy(j).start()
 
     def send_a2(j):
-        return rcopy(s2a.at[ym(j)], r2a.at[y], s2a_s.at[j], s2a_r.at[y], col=cl(x, ym(j)))
+        return rcopy(s2a.at[ym(j)], r2a.at[y], s2a_s, s2a_r, col=cl(x, ym(j)))
 
     def send_b2(j):
-        return rcopy(s2b.at[xm(j)], r2b.at[x], s2b_s.at[j], s2b_r.at[x], col=cl(xm(j), y))
+        return rcopy(s2b.at[xm(j)], r2b.at[x], s2b_s, s2b_r, col=cl(xm(j), y))
 
     def sum_a(yy):
         return (
@@ -338,7 +337,7 @@
     def wait_b(xx):
         for j in range(1, NY):
             part = rb.at[ym(j), xx]
-            rcopy(part, part, sb_s.at[j, xx], sb_r.at[ym(j), xx], col=me_c).wait_recv()
+            rcopy(part, part, sb_s, sb_r.at[ym(j), xx], col=me_c).wait_recv()
 
     def stage_b2(j, carry):
         wait_b(xm(j))
@@ -347,8 +346,7 @@
         return carry
 
     lax.fori_loop(1, NX, stage_b2, 0)
-    for j in range(1, NX):
-        rcopy(ra.at[xm(j)], ra.at[xm(j)], sa_s.at[j], sa_r.at[xm(j)], col=me_c).wait_recv()
+    rcopy(ra.at[0:3], ra.at[0:3], sa_s, sa_r, row=partner).wait_recv()
 
     def stage_a2(j, carry):
         s2a[ym(j)] = sum_a(ym(j)).astype(BF16)
@@ -361,8 +359,7 @@
     nsum[:, 128:256] = sum_b(x)
 
     dg3[y] = dg2[y]
-    for j in range(1, NY):
-        rcopy(dg3.at[ym(j)], dg3.at[ym(j)], dgy_s.at[j], dgy_r.at[ym(j)], col=me_c).wait_recv()
+    rcopy(dg3.at[0:3], dg3.at[0:3], dgy_s, dgy_r, row=partner).wait_recv()
     degree = dg3[0] + dg3[1] + dg3[2] + dg3[3]
     inv_lane = 1.0 / jnp.sqrt(degree + 1.0)
     eye = line == lane
@@ -374,13 +371,11 @@
         axis=0,
     )
 
-    for j in range(1, NY):
-        rcopy(r2a.at[ym(j)], r2a.at[ym(j)], s2a_s.at[j], s2a_r.at[ym(j)], col=me_c).wait_recv()
+    rcopy(r2a.at[0:3], r2a.at[0:3], s2a_s, s2a_r, row=partner).wait_recv()
     nsum[:, 0:128] += (
         r2a[ym(1)].astype(F32) + r2a[ym(2)].astype(F32) + r2a[ym(3)].astype(F32)
     )
-    for j in range(1, NX):
-        rcopy(r2b.at[xm(j)], r2b.at[xm(j)], s2b_s.at[j], s2b_r.at[xm(j)], col=me_c).wait_recv()
+    rcopy(r2b.at[0:3], r2b.at[0:3], s2b_s, s2b_r, row=partner).wait_recv()
     nsum[:, 128:256] += (
         r2b[xm(1)].astype(F32) + r2b[xm(2)].astype(F32) + r2b[xm(3)].astype(F32)
     )
@@ -401,21 +396,21 @@
     dtab[me_c, 1] = gsum[:, 128:256]
 
     def full_x(j):
-        return rcopy(dtab.at[me_c], dtab.at[me_c], df_s.at[j], df_r.at[me_c], col=cl(xm(j), y))
+        return rcopy(dtab.at[me_c], dtab.at[me_c], df_s, df_r.at[me_c], col=cl(xm(j), y))
 
     def full_y(j):
-        return rcopy(dtab.at[me_c], dtab.at[me_c], df_s.at[3 + j], df_r.at[me_c], col=cl(x, ym(j)))
+        return rcopy(dtab.at[me_c], dtab.at[me_c], df_s, df_r.at[me_c], col=cl(x, ym(j)))
 
     def half_a(jx, jy):
         part = dtab.at[cl(xm(jx), y), 0]
         return rcopy(
-            part, part, da_s.at[jx * 4 + jy], da_r.at[cl(xm(jx), y)], col=cl(x, ym(jy))
+            part, part, da_s, da_r.at[cl(xm(jx), y)], col=cl(x, ym(jy))
         )
 
     def half_b(jx, jy):
         part = dtab.at[cl(x, ym(jy)), 1]
         return rcopy(
-            part, part, db_s.at[jx * 4 + jy], db_r.at[cl(x, ym(jy))], col=cl(xm(jx), y)
+            part, part, db_s, db_r.at[cl(x, ym(jy))], col=cl(xm(jx), y)
         )
 
     def start_full(j, carry):
@@ -439,18 +434,18 @@
 
     def send_w1(j):
         zz = zm(z + j)
-        return rcopy(w1s.at[zz], w1r.at[z], w1_s.at[j], w1_r.at[z], row=rw(zz, k))
+        return rcopy(w1s.at[zz], w1r.at[z], w1_s, w1_r, row=rw(zz, k))
 
     def send_w2(j):
-        return rcopy(wz.at[z], wz.at[z], w2_s.at[j], w2_r.at[z], row=rw(z + j, k))
+        return rcopy(wz.at[z], wz.at[z], w2_s, w2_r, row=rw(z + j, k))
 
     def send_x1(j):
         c = (me_c + j) % 16
-        return rcopy(x1s.at[c], x1r.at[me_c], x1_s.at[j], x1_r.at[me_c], col=c)
+        return rcopy(x1s.at[c], x1r.at[me_c], x1_s, x1_r, col=c)
 
     def send_x2(j):
         part = gfin.at[k, me_c]
-        return rcopy(part, part, x2_s.at[j], x2_r.at[me_c], col=(me_c + j) % 16)
+        return rcopy(part, part, x2_s, x2_r, col=(me_c + j) % 16)
 
     def send_pf():
         return rcopy(gfin.at[k], gfin.at[k], pf_s, pf_r, row=partner)
@@ -459,7 +454,7 @@
 
     def take_x(jx):
         c = cl(xm(jx), y)
-        rcopy(dtab.at[c], dtab.at[c], df_s.at[jx], df_r.at[c], col=me_c).wait_recv()
+        rcopy(dtab.at[c], dtab.at[c], df_s, df_r.at[c], col=me_c).wait_recv()
 
         def go(jy, carry):
             half_a(jx, jy).start()
@@ -469,7 +464,7 @@
 
     def take_y(jy):
         c = cl(x, ym(jy))
-        rcopy(dtab.at[c], dtab.at[c], df_s.at[jy], df_r.at[c], col=me_c).wait_recv()
+        rcopy(dtab.at[c], dtab.at[c], df_s, df_r.at[c], col=me_c).wait_recv()
 
         def go(jx, carry):
             half_b(jx, jy).start()
@@ -479,26 +474,26 @@
 
     def take_rest(c):
         part = dtab.at[c, 0]
-        rcopy(part, part, da_s.at[0], da_r.at[c], col=me_c).wait_recv()
+        rcopy(part, part, da_s, da_r.at[c], col=me_c).wait_recv()
         part = dtab.at[c, 1]
-        rcopy(part, part, db_s.at[0], db_r.at[c], col=me_c).wait_recv()
-
+        rcopy(part, part, db_s, db_r.at[c], col=me_c).wait_recv()
+
+    send_w0().wait_recv()
+    gwb[k] = gwb[k] + gwr[...]
+
+    def split_z(j, carry):
+        w1s[j, 0:32, :] = gwb[k, pl.ds(pl.multiple_of(j * 32, 32), 32), :].astype(BF16)
+        w1s[j, 32:48, :] = jnp.concatenate([gwb[k, 256:264, :]] * 2, axis=0).astype(BF16)
+        return carry
+
+    lax.fori_loop(0, NZ, split_z, 0)
+    for j in range(1, NZ):
+        send_w1(j).start()
+    w1r[z] = w1s[z]
     take_x(1)
     take_y(1)
     take_x(3)
     take_y(3)
-    send_w0().wait_recv()
-    gwb[k] = gwb[k] + gwr[...]
-
-    def split_z(j, carry):
-        w1s[j, 0:32, :] = gwb[k, pl.ds(pl.multiple_of(j * 32, 32), 32), :].astype(BF16)
-        w1s[j, 32:48, :] = jnp.concatenate([gwb[k, 256:264, :]] * 2, axis=0).astype(BF16)
-        return carry
-
-    lax.fori_loop(0, NZ, split_z, 0)
-    for j in range(1, NZ):
-        send_w1(j).start()
-    w1r[z] = w1s[z]
 
     def order(q):
         m = q - 7
@@ -514,9 +509,7 @@
 
         @pl.when(g == 3)
         def _():
-            for j in range(1, NZ):
-                zz = zm(z + j)
-                rcopy(w1r.at[zz], w1r.at[zz], w1_s.at[j], w1_r.at[zz], row=me_r).wait_recv()
+            rcopy(w1r.at[0:7], w1r.at[0:7], w1_s, w1_r, row=partner).wait_recv()
             tot = w1r[0].astype(F32)
             for j in range(1, NZ):
                 tot = tot + w1r[j].astype(F32)
@@ -545,7 +538,7 @@
         return acc[pl.ds(pl.multiple_of(rw(zz, kk) * 256, 256), 256), :]
 
     def send_p(zz):
-        return rcopy(psend.at[zz], precv.at[zz], p_s.at[zz], p_r.at[zz], row=partner)
+        return rcopy(psend.at[zz], precv.at[zz], p_s, p_r.at[zz], row=partner)
 
     def put_p(zz):
         psend[zz] = chunk(zz, kp).astype(BF16)
@@ -564,20 +557,20 @@
 
     def send_e3(i, h):
         return rcopy(
-            esend.at[i, h], e3.at[i, h], e3_s.at[i, h], e3_r.at[i, h], row=rw(z + 1 - 2 * i, k)
+            esend.at[i, h], e3.at[i, h], e_s, e3_r.at[i, h], row=rw(z + 1 - 2 * i, k)
         )
 
     def send_e4(i):
-        return rcopy(esend.at[2, i], e4.at[i], e4_s.at[i], e4_r.at[i], row=rw(z + 2 - 4 * i, k))
+        return rcopy(esend.at[2, i], e4.at[i], e_s, e4_r.at[i], row=rw(z + 2 - 4 * i, k))
 
     def send_f1(i, h):
         return rcopy(
-            esend.at[3 + i, h], f1.at[i, h], f1_s.at[i, h], f1_r.at[i, h], row=rw(z + 1 - 2 * i, k)
+            esend.at[3 + i, h], f1.at[i, h], e_s, f1_r.at[i, h], row=rw(z + 1 - 2 * i, k)
         )
 
     def send_f2(i, h):
         return rcopy(
-            esend.at[5 + i, h], f2.at[i, h], f2_s.at[i, h], f2_r.at[i, h], row=rw(z + 2 - 4 * i, k)
+            esend.at[5 + i, h], f2.at[i, h], e_s, f2_r.at[i, h], row=rw(z + 2 - 4 * i, k)
         )
 
     def finish_at(j, carry):
@@ -615,9 +608,7 @@
 
     lax.fori_loop(0, 2, to_next, 0)
 
-    for j in range(1, NZ):
-        zz = zm(z + j)
-        rcopy(wz.at[zz], wz.at[zz], w2_s.at[j], w2_r.at[zz], row=me_r).wait_recv()
+    rcopy(wz.at[0:7], wz.at[0:7], w2_s, w2_r, row=partner).wait_recv()
 
     def split_c(i, carry):
         for u in range(2):
@@ -656,12 +647,7 @@
 
     lax.fori_loop(0, 2, to_second, 0)
 
-    def wait_x1(j, carry):
-        c = (me_c + j) % 16
-        rcopy(x1r.at[c], x1r.at[c], x1_s.at[j], x1_r.at[c], col=me_c).wait_recv()
-        return carry
-
-    lax.fori_loop(1, NX * NY, wait_x1, 0)
+    rcopy(x1r.at[0:15], x1r.at[0:15], x1_s, x1_r, row=partner).wait_recv()
     tot = x1r[0]
     for c in range(1, NX * NY):
         tot = tot + x1r[c]
@@ -681,13 +667,7 @@
             own_part(z, h) + f1[0, h].astype(F32) + f1[1, h].astype(F32)
         )
 
-    def wait_x2(j, carry):
-        c = (me_c + j) % 16
-        part = gfin.at[k, c]
-        rcopy(part, part, x2_s.at[j], x2_r.at[c], col=me_c).wait_recv()
-        return carry
-
-    lax.fori_loop(1, NX * NY, wait_x2, 0)
+    rcopy(gfin.at[k, 0:15], gfin.at[k, 0:15], x2_s, x2_r, row=partner).wait_recv()
     send_pf().start()
     for h in range(2):
         for i in range(2):
@@ -699,49 +679,28 @@
     g_ws[...] = gfin[0].reshape(256, 256)
     g_wn[...] = gfin[1].reshape(256, 256)
 
-    def drain_h(h, carry):
-        for i in range(7):
-            ag_send(own(h), me_r, h, i, 1).wait_send()
-        for j in range(NZ):
-            ag_partner(own(h), j * 2, h).wait_send()
-        for i in range(2):
-            send_e3(i, h).wait_send()
-            send_f1(i, h).wait_send()
-            send_f2(i, h).wait_send()
-        send_e4(h).wait_send()
-        return carry
-
-    lax.fori_loop(0, 2, drain_h, 0)
+    def sent(buf, sem):
+        rcopy(buf, buf, sem, ag_r.at[0, 0], row=partner).wait_send()
+
+    sent(tab.at[0:7], ag_s)
+    sent(tab.at[0:8], ag_sp)
+    sent(sa.at[0:3], sa_s)
+    sent(sb.at[0:3], sb_s)
+    sent(s2a.at[0:3], s2a_s)
+    sent(s2b.at[0:3], s2b_s)
+    sent(dg0.at[0:3], dgx_s)
+    sent(dg2.at[0:3], dgy_s)
+    sent(dtab.at[0:6], df_s)
+    sent(dtab.at[0:9, 0], da_s)
+    sent(dtab.at[0:9, 1], db_s)
+    sent(w1s.at[0:7], w1_s)
+    sent(wz.at[0:7], w2_s)
+    sent(x1s.at[0:15], x1_s)
+    sent(gfin.at[k, 0:15], x2_s)
+    sent(psend, p_s)
+    sent(esend, e_s)
     send_w0().wait_send()
     send_pf().wait_send()
-    send_p(0).wait_send()
-
-    def drain_z(j, carry):
-        send_p(j).wait_send()
-        send_w1(j).wait_send()
-        send_w2(j).wait_send()
-        return carry
-
-    lax.fori_loop(1, NZ, drain_z, 0)
-
-    def drain_c(j, carry):
-        send_x1(j).wait_send()
-        send_x2(j).wait_send()
-        return carry
-
-    lax.fori_loop(1, NX * NY, drain_c, 0)
-
-    def drain_xy(j, carry):
-        for copy in (send_a(j), send_a2(j), send_b2(j), send_dx(j), send_dy(j), full_x(j), full_y(j)):
-            copy.wait_send()
-        for i in range(1, 4):
-            half_a(j, i).wait_send()
-            half_b(j, i).wait_send()
-        for i in range(4):
-            send_b(j, i).wait_send()
-        return carry
-
-    lax.fori_loop(1, 4, drain_xy, 0)
 
 
 def hand_over(*refs):
@@ -814,28 +773,29 @@
             dma((16,)),
             dma,
             dma((16, 2)),
-            dma((7, 2)),
-            dma((NZ, 2)),
-            dma((4,)), dma((4,)),
-            dma((4, 4)), dma((4, 4)),
-            dma((4,)), dma((4,)),
-            dma((4,)), dma((4,)),
-            dma((4,)), dma((4,)),
-            dma((4,)), dma((4,)),
-            dma((7,)), dma((16,)),
-            dma((16,)), dma((16,)),
-            dma((16,)), dma((16,)),
-            dma, dma,
-            dma((NZ,)), dma((NZ,)),
-            dma((NZ,)), dma((NZ,)),
-            dma((16,)), dma((16,)),
-            dma((16,)), dma((16,)),
-            dma, dma,
-            dma((NZ,)), dma((NZ,)),
-            dma((2, 2)), dma((2, 2)),
-            dma((2,)), dma((2,)),
-            dma((2, 2)), dma((2, 2)),
-            dma((2, 2)), dma((2, 2)),
+            dma,
+            dma,
+            dma, dma,
+            dma, dma((4, 4)),
+            dma, dma,
+            dma, dma,
+            dma, dma,
+            dma, dma,
+            dma, dma((16,)),
+            dma, dma((16,)),
+            dma, dma((16,)),
+            dma, dma,
+            dma, dma,
+            dma, dma,
+            dma, dma,
+            dma, dma,
+            dma, dma,
+            dma, dma((NZ,)),
+            dma,
+            dma((2, 2)),
+            dma((2,)),
+            dma((2, 2)),
+            dma((2, 2)),
         ],
         compiler_params=pltpu.CompilerParams(
             collective_id=0, has_side_effects=True, vmem_limit_bytes=56 * 1024 * 1024

time: 103 us -> 100 us (0.971)
  Pallas kernels: 102 us -> 99.1 us
    pallas_call x1, Pallas kernels: 99.8 us -> 96.9 us  [body(): pl.pallas_call(functools.partial(kernel, scale), out_shape=(jax.ShapeDtyp...]
where the time goes in v3:
time: 100 us
  Pallas kernels  99.1 us (99%)
  between operations  1.29 us (1%)
    pallas_call x1, Pallas kernels, body(): pl.pallas_call(functools.partial(kernel, scale), out_shape=(jax.ShapeDtyp...  96.9 us
    pallas_call x1, Pallas kernels, body(): pl.pallas_call(hand_over, out_shape=tuple((jax.ShapeDtypeStruct(o.shape,...  2.14 us

profile of v3, /device:TPU:1, one launch (start us, length us, event | category | flops | bytes accessed | tf_op | source)
XLA Modules:
  0.0 100.4 jit_solution(12371566236896678130)
XLA Ops:
  1.3 96.9 %shard_map.145 = (bf16[256,256]{1,0:T(8,128)(2,1)}, bf16[256,256]{1,0:T(8,128)(2,1)}, bf16[256,256]{1,0:T(8,128)(2,1)}, f32[256,256]{1,0:T(8,128)}, f32[256,256]{1,0:T(8,128)}, /*index=5*/f32[1,256]{1,0:T(1,128)}) custom-call(s32[1,128]{1,0:T(1,128)} %bitcast.6, s32[1,128]{1,0:T(1,128)} %bitcast.9, s32[1,1]{1,0:T(1,128)S(6)} %copy.16.live_at.live, ...), custom_call_target="tpu_custom_call" | custom-call | tf_op jit(solution)/shard_map/pallas_call | solution.py:721
  98.2 2.1 %shard_map.146 = (bf16[256,256]{1,0:T(8,128)(2,1)}, bf16[256,256]{1,0:T(8,128)(2,1)}, bf16[256,256]{1,0:T(8,128)(2,1)}, f32[256,256]{1,0:T(8,128)}, f32[256,256]{1,0:T(8,128)}, /*index=5*/f32[1,256]{1,0:T(1,128)}) custom-call(bf16[256,256]{1,0:T(8,128)(2,1)} %get-tuple-element.18.refs_0_, bf16[256,256]{1,0:T(8,128)(2,1)} %get-tuple-element.19.refs_1_, ...), custom_call_target="tpu_custom_call" | custom-call | tf_op jit(solution)/shard_map/pallas_call | solution.py:807

commit v4 on v3

--- a/solution.py
+++ b/solution.py
@@ -24,11 +24,11 @@
 
 def kernel(
     scale,
-    dst_at, src_at, live_at, dst_ids, live, emb, feat, w_self, w_neigh, bias, cot, counts,
+    dst_at, src_at, live_at, dst_ids, live, emb, feat_in, w_self_in, w_neigh_in, bias_in, cot_in, counts,
     layer_out, grad_self, grad_source, g_ws, g_wn, g_b,
-    sel, selv, stage, cnt, cnt_t, acc, tab, sa, sb, ra, rb, s2a, s2b, r2a, r2b, nsum, rsum, dg0, dg1, dg2,
+    feat, w_self, w_neigh, bias, cot, sel, selv, stage, cnt, cnt_t, acc, tab, sa, sb, ra, rb, s2a, s2b, r2a, r2b, nsum, rsum, dg0, dg1, dg2,
     dg3, agg, gpre, dtab, gwb, gwr, w1s, w1r, wz, x1s, x1r, gfin, psend, precv, esend, e3, e4, f1, f2,
-    csem, selsem, ag_r, ag_s, ag_sp, sa_s, sa_r, sb_s, sb_r, s2a_s, s2a_r, s2b_s, s2b_r,
+    isem, csem, selsem, ag_r, ag_s, ag_sp, sa_s, sa_r, sb_s, sb_r, s2a_s, s2a_r, s2b_s, s2b_r,
     dgx_s, dgx_r, dgy_s, dgy_r, df_s, df_r, da_s, da_r, db_s, db_r,
     w0_s, w0_r, w1_s, w1_r, w2_s, w2_r, x1_s, x1_r, x2_s, x2_r, pf_s, pf_r,
     p_s, p_r, e_s, e3_r, e4_r, f1_r, f2_r,
@@ -126,6 +126,14 @@
     for h in range(2):
         ag_partner(own(h), me_r, h).start()
     lax.fori_loop(0, 16, start_counts, 0)
+    inputs = [
+        pltpu.make_async_copy(a, b, isem.at[i])
+        for i, (a, b) in enumerate(
+            ((feat_in, feat), (w_self_in, w_self), (w_neigh_in, w_neigh), (bias_in, bias), (cot_in, cot))
+        )
+    ]
+    for copy in inputs:
+        copy.start()
     tab[me_r, 0] = emb[0:128]
     tab[me_r, 1] = emb[128:256]
     cnt[ZERO_SLOT] = jnp.zeros((128, 128), BF16)
@@ -213,13 +221,15 @@
             take(rw(z - 1, k))
             take(rw(z + 1, k))
 
-        @pl.when(t >= 2)
+        @pl.when(t == 2)
         def _():
             take(rw(z - 3, k))
             take(rw(z + 3, k))
             take(rw(z + 4, k))
 
-        lax.fori_loop(t * 8, t * 8 + 8, transpose, 0)
+        @pl.when(t < 2)
+        def _():
+            lax.fori_loop(16 + t * 8, 24 + t * 8, transpose, 0)
 
         @pl.when(t == 0)
         def _():
@@ -236,8 +246,16 @@
         s0 = rw(z - dz, (k + (t // 2) * (3 - t)) % 2)
         s1 = rw(z + dz, (k + (t + 1) % 2) % 2)
         spmm(cnt, fwd_pick, source_rows, (s0, s1))
-        return carry
-
+
+        @pl.when(t == 3)
+        def _():
+            take(rw(z - 3, k))
+            take(rw(z + 3, k))
+            take(rw(z + 4, k))
+
+        return carry
+
+    lax.fori_loop(0, 16, transpose, 0)
     lax.fori_loop(0, 4, ag_step, 0)
 
     hot = ((line // 8) * 2 + line % 8 == dst_ids[...]) & (line % 8 < 2) & used
@@ -265,8 +283,10 @@
             ag_wait(rw(z + dz, kp), h)
         ag_wait(rw(z - 4, kp), h)
 
-    def send_a(j):
-        return rcopy(sa.at[xm(j)], ra.at[x], sa_s, sa_r, col=cl(xm(j), y))
+    def send_a(jx, yy):
+        return rcopy(
+            sa.at[xm(jx), yy], ra.at[x, yy], sa_s, sa_r.at[x, yy], col=cl(xm(jx), y)
+        )
 
     def send_b(jy, xx):
         return rcopy(
@@ -299,7 +319,8 @@
 
         @pl.when(jx < 4)
         def _():
-            send_a(jx).start()
+            for j in range(1, NY + 1):
+                send_a(jx, ym(j)).start()
 
         for j in range(1, NY):
             send_b(j, xx).start()
@@ -346,14 +367,20 @@
         return carry
 
     lax.fori_loop(1, NX, stage_b2, 0)
-    rcopy(ra.at[0:3], ra.at[0:3], sa_s, sa_r, row=partner).wait_recv()
+
+    def wait_a(yy):
+        for j in range(1, NX):
+            part = ra.at[xm(j), yy]
+            rcopy(part, part, sa_s, sa_r.at[xm(j), yy], col=me_c).wait_recv()
 
     def stage_a2(j, carry):
+        wait_a(ym(j))
         s2a[ym(j)] = sum_a(ym(j)).astype(BF16)
         send_a2(j).start()
         return carry
 
     lax.fori_loop(1, NY, stage_a2, 0)
+    wait_a(y)
     wait_b(x)
     nsum[:, 0:128] = sum_a(y)
     nsum[:, 128:256] = sum_b(x)
@@ -380,6 +407,8 @@
         r2b[xm(1)].astype(F32) + r2b[xm(2)].astype(F32) + r2b[xm(3)].astype(F32)
     )
 
+    for copy in inputs:
+        copy.wait()
     agg[...] = (nsum[...] * inv_col).astype(BF16)
     pre = (
         jnp.dot(feat[...], w_self[...], preferred_element_type=F32)
@@ -728,9 +757,14 @@
             jax.ShapeDtypeStruct((256, 256), F32),
             jax.ShapeDtypeStruct((1, 256), F32),
         ),
-        in_specs=[pl.BlockSpec(memory_space=pltpu.SMEM)] * 3 + [vm] * 8 + [pl.BlockSpec(memory_space=pl.ANY)],
+        in_specs=[pl.BlockSpec(memory_space=pltpu.SMEM)] * 3 + [vm] * 3 + [pl.BlockSpec(memory_space=pl.ANY)] * 6,
         out_specs=(vm,) * 6,
         scratch_shapes=[
+            v((256, 256), BF16),
+            v((256, 256), BF16),
+            v((256, 256), BF16),
+            v((1, 256), F32),
+            v((256, 256), BF16),
             pltpu.SMEM((NB, 128), jnp.int32),
             v((NB, 128), jnp.int32),
             v((SLOTS, 128, 128), jnp.int32),
@@ -770,12 +804,13 @@
             v((2, 128, 256), BF16),
             v((2, 2, 128, 256), BF16),
             v((2, 2, 128, 256), BF16),
+            dma((5,)),
             dma((16,)),
             dma,
             dma((16, 2)),
             dma,
             dma,
-            dma, dma,
+            dma, dma((4, 4)),
             dma, dma((4, 4)),
             dma, dma,
             dma, dma,

time: 100 us -> 98.8 us (0.988)
  Pallas kernels: 99.1 us -> 97.4 us
    pallas_call x1, Pallas kernels: 96.9 us -> 95.3 us  [body(): pl.pallas_call(functools.partial(kernel, scale), out_shape=(jax.ShapeDtyp...]
where the time goes in v4:
time: 98.8 us; the launch traced here: 98.7 us
  Pallas kernels  97.4 us (99%)
  between operations  1.29 us (1%)
    pallas_call x1, Pallas kernels, body(): pl.pallas_call(functools.partial(kernel, scale), out_shape=(jax.ShapeDtyp...  95.3 us
    pallas_call x1, Pallas kernels, body(): pl.pallas_call(hand_over, out_shape=tuple((jax.ShapeDtypeStruct(o.shape,...  2.14 us

profile of v4, /device:TPU:1, one launch (start us, length us, event | category | flops | bytes accessed | tf_op | source)
XLA Modules:
  0.0 98.7 jit_solution(6787267369148346732)
XLA Ops:
  1.3 95.3 %shard_map.145 = (bf16[256,256]{1,0:T(8,128)(2,1)}, bf16[256,256]{1,0:T(8,128)(2,1)}, bf16[256,256]{1,0:T(8,128)(2,1)}, f32[256,256]{1,0:T(8,128)}, f32[256,256]{1,0:T(8,128)}, /*index=5*/f32[1,256]{1,0:T(1,128)}) custom-call(s32[1,128]{1,0:T(1,128)} %bitcast.6, s32[1,128]{1,0:T(1,128)} %bitcast.9, s32[1,1]{1,0:T(1,128)S(6)} %copy.16.live_at.live, ...), custom_call_target="tpu_custom_call" | custom-call | tf_op jit(solution)/shard_map/pallas_call | solution.py:750
  96.6 2.1 %shard_map.146 = (bf16[256,256]{1,0:T(8,128)(2,1)}, bf16[256,256]{1,0:T(8,128)(2,1)}, bf16[256,256]{1,0:T(8,128)(2,1)}, f32[256,256]{1,0:T(8,128)}, f32[256,256]{1,0:T(8,128)}, /*index=5*/f32[1,256]{1,0:T(1,128)}) custom-call(bf16[256,256]{1,0:T(8,128)(2,1)} %get-tuple-element.18.refs_0_, bf16[256,256]{1,0:T(8,128)(2,1)} %get-tuple-element.19.refs_1_, ...), custom_call_target="tpu_custom_call" | custom-call | tf_op jit(solution)/shard_map/pallas_call | solution.py:842

commit v5 on v4

--- a/solution.py
+++ b/solution.py
@@ -637,23 +637,6 @@
 
     lax.fori_loop(0, 2, to_next, 0)
 
-    rcopy(wz.at[0:7], wz.at[0:7], w2_s, w2_r, row=partner).wait_recv()
-
-    def split_c(i, carry):
-        for u in range(2):
-            x1s[2 * i + u, 0:16, :] = wz[i, u * 16 : u * 16 + 16, :]
-            x1s[2 * i + u, 16:24, :] = gwb[k, 256:264, :]
-        return carry
-
-    lax.fori_loop(0, NZ, split_c, 0)
-    x1r[me_c] = x1s[me_c]
-
-    def start_x1(j, carry):
-        send_x1(j).start()
-        return carry
-
-    lax.fori_loop(1, NX * NY, start_x1, 0)
-
     def to_second(i, carry):
         zz = zm(z + 2 + 4 * i)
         send_p(zz).wait_recv()
@@ -675,6 +658,23 @@
         return carry
 
     lax.fori_loop(0, 2, to_second, 0)
+
+    rcopy(wz.at[0:7], wz.at[0:7], w2_s, w2_r, row=partner).wait_recv()
+
+    def split_c(i, carry):
+        for u in range(2):
+            x1s[2 * i + u, 0:16, :] = wz[i, u * 16 : u * 16 + 16, :]
+            x1s[2 * i + u, 16:24, :] = gwb[k, 256:264, :]
+        return carry
+
+    lax.fori_loop(0, NZ, split_c, 0)
+    x1r[me_c] = x1s[me_c]
+
+    def start_x1(j, carry):
+        send_x1(j).start()
+        return carry
+
+    lax.fori_loop(1, NX * NY, start_x1, 0)
 
     rcopy(x1r.at[0:15], x1r.at[0:15], x1_s, x1_r, row=partner).wait_recv()
     tot = x1r[0]

time: 98.8 us -> 104 us (1.053)
  Pallas kernels: 97.4 us -> 102 us
    pallas_call x1, Pallas kernels: 95.3 us -> 100 us  [body(): pl.pallas_call(functools.partial(kernel, scale), out_shape=(jax.ShapeDtyp...]
where the time goes in v5:
time: 104 us
  Pallas kernels  102 us (98%)
  between operations  1.29 us (1%)
    pallas_call x1, Pallas kernels, body(): pl.pallas_call(functools.partial(kernel, scale), out_shape=(jax.ShapeDtyp...  100 us
    pallas_call x1, Pallas kernels, body(): pl.pallas_call(hand_over, out_shape=tuple((jax.ShapeDtypeStruct(o.shape,...  2.14 us

profile of v5, /device:TPU:1, one launch (start us, length us, event | category | flops | bytes accessed | tf_op | source)
XLA Modules:
  0.0 103.7 jit_solution(14505533068950986569)
XLA Ops:
  1.3 100.3 %shard_map.145 = (bf16[256,256]{1,0:T(8,128)(2,1)}, bf16[256,256]{1,0:T(8,128)(2,1)}, bf16[256,256]{1,0:T(8,128)(2,1)}, f32[256,256]{1,0:T(8,128)}, f32[256,256]{1,0:T(8,128)}, /*index=5*/f32[1,256]{1,0:T(1,128)}) custom-call(s32[1,128]{1,0:T(1,128)} %bitcast.6, s32[1,128]{1,0:T(1,128)} %bitcast.9, s32[1,1]{1,0:T(1,128)S(6)} %copy.16.live_at.live, ...), custom_call_target="tpu_custom_call" | custom-call | tf_op jit(solution)/shard_map/pallas_call | solution.py:750
  101.6 2.1 %shard_map.146 = (bf16[256,256]{1,0:T(8,128)(2,1)}, bf16[256,256]{1,0:T(8,128)(2,1)}, bf16[256,256]{1,0:T(8,128)(2,1)}, f32[256,256]{1,0:T(8,128)}, f32[256,256]{1,0:T(8,128)}, /*index=5*/f32[1,256]{1,0:T(1,128)}) custom-call(bf16[256,256]{1,0:T(8,128)(2,1)} %get-tuple-element.18.refs_0_, bf16[256,256]{1,0:T(8,128)(2,1)} %get-tuple-element.19.refs_1_, ...), custom_call_target="tpu_custom_call" | custom-call | tf_op jit(solution)/shard_map/pallas_call | solution.py:842
